TPU v7x, 128 devices: a whole 4x4x4 slice. The times are simulated.
128 devices in a mesh: dp: 8 (over y, x_lo), ctx: 16 (over z, x_hi, core).
Axes of the slice: x: 4 (x_hi: 2, x_lo: 2; x = x_hi * 2 + x_lo), y: 4, z: 4, core: 2. Of those that a mesh axis runs over, the one named last changes fastest.
Arguments:
- queries: bfloat16 [24576, 4096], P(('dp', 'ctx')), may hold values from -6.5 to 6.5
- keys: bfloat16 [24576, 512], P(('dp', 'ctx')), may hold values from -4 to 4
- values: bfloat16 [24576, 512], P(('dp', 'ctx')), may hold values from -6 to 6
- out_grad: bfloat16 [24576, 4096], P(('dp', 'ctx')), may hold values from -6 to 6
- hidden: bfloat16 [24576, 8192], P(('dp', 'ctx')), may hold values from -24 to 24
Outputs:
- query_grad: bfloat16 [24576, 4096], P(('dp', 'ctx'))
- key_grad: bfloat16 [24576, 512], P(('dp', 'ctx'))
- value_grad: bfloat16 [24576, 512], P(('dp', 'ctx'))
- key_weight_grad: float32 [8192, 512], P(('dp', 'ctx'))
- value_weight_grad: float32 [8192, 512], P(('dp', 'ctx'))
All inputs are finite; a program needn't handle non-finite values.
Results may differ from a plain program's by a relative error of at most 0.02.
Values may be sent and summed in bfloat16 or wider, within the bound.
A program may use at most 256 MiB of HBM per device.

v0:
```python
import math

import jax
import jax.numpy as jnp
from jax import lax
from jax.sharding import PartitionSpec as P

HD = 128
BLOCK = 512


def on_device(queries, keys, values, out_grad, hidden):
    tok_rows = queries.shape[0]
    ctx_size = lax.axis_size("ctx")
    kv_heads = keys.shape[1] // HD
    replicas = ctx_size // kv_heads
    score_scale = 1.0 / math.sqrt(HD)
    query_slab, grad_slab = (
        lax.all_to_all(queries, "ctx", split_axis=1, concat_axis=0, tiled=True),
        lax.all_to_all(out_grad, "ctx", split_axis=1, concat_axis=0, tiled=True),
    )
    seq_len = query_slab.shape[0]
    per_dev = query_slab.shape[1] // HD
    key_all, value_all = (
        lax.all_gather(keys, "ctx", axis=0, tiled=True),
        lax.all_gather(values, "ctx", axis=0, tiled=True),
    )
    offset = lax.axis_index("ctx") // replicas * HD
    key_head = lax.dynamic_slice_in_dim(key_all, offset, HD, 1)
    value_head = lax.dynamic_slice_in_dim(value_all, offset, HD, 1)
    query_heads = query_slab.reshape(seq_len, per_dev, HD)
    grad_heads = grad_slab.reshape(seq_len, per_dev, HD)
    key_total = jnp.zeros((seq_len, HD), jnp.float32)
    value_total = jnp.zeros((seq_len, HD), jnp.float32)
    pieces = []
    for block_index in range(seq_len // BLOCK):
        low_row = block_index * BLOCK
        high_row = low_row + BLOCK
        query_block = query_heads[low_row:high_row]
        grad_block = grad_heads[low_row:high_row]
        key_block = key_head[:high_row]
        value_block = value_head[:high_row]
        scores = (
            jnp.einsum("qhd,kd->hqk", query_block, key_block, preferred_element_type=jnp.float32)
            * score_scale
        )
        row_ids = lax.broadcasted_iota(jnp.int32, (BLOCK, high_row), 0) + low_row
        col_ids = lax.broadcasted_iota(jnp.int32, (BLOCK, high_row), 1)
        scores = jnp.where((col_ids <= row_ids)[None], scores, -jnp.inf)
        row_max = jnp.max(scores, axis=2, keepdims=True)
        exponent = jnp.exp(scores - row_max)
        probability = exponent / jnp.sum(exponent, axis=2, keepdims=True)
        prob_low = probability.astype(jnp.bfloat16)
        attended = jnp.einsum(
            "hqk,kd->hqd", prob_low, value_block, preferred_element_type=jnp.float32
        )
        grad_major = jnp.transpose(grad_block, (1, 0, 2)).astype(jnp.float32)
        row_delta = jnp.sum(grad_major * attended, axis=2, keepdims=True)
        prob_grad = jnp.einsum(
            "qhd,kd->hqk", grad_block, value_block, preferred_element_type=jnp.float32
        )
        score_grad = (probability * (prob_grad - row_delta)).astype(jnp.bfloat16)
        query_piece = (
            jnp.einsum("hqk,kd->qhd", score_grad, key_block, preferred_element_type=jnp.float32)
            * score_scale
        )
        pieces.append(query_piece.astype(jnp.bfloat16))
        key_total = key_total.at[:high_row].add(
            jnp.einsum("hqk,qhd->kd", score_grad, query_block, preferred_element_type=jnp.float32)
            * score_scale
        )
        value_total = value_total.at[:high_row].add(
            jnp.einsum("hqk,qhd->kd", prob_low, grad_block, preferred_element_type=jnp.float32)
        )
    query_local = jnp.concatenate(pieces, 0).reshape(seq_len, per_dev * HD)
    query_grad = lax.all_to_all(query_local, "ctx", split_axis=0, concat_axis=1, tiled=True)
    key_slots, value_slots = (
        lax.all_to_all(
            key_total.astype(jnp.bfloat16), "ctx", split_axis=0, concat_axis=1, tiled=True
        ),
        lax.all_to_all(
            value_total.astype(jnp.bfloat16), "ctx", split_axis=0, concat_axis=1, tiled=True
        ),
    )

    def fold_slots(slot_array):
        summed = jnp.sum(
            slot_array.reshape(tok_rows, kv_heads, replicas, HD).astype(jnp.float32), axis=2
        )
        return summed.astype(jnp.bfloat16).reshape(tok_rows, kv_heads * HD)

    key_grad = fold_slots(key_slots)
    value_grad = fold_slots(value_slots)
    kv_grads = jnp.concatenate([key_grad, value_grad], 1)
    contract = (((0,), (0,)), ((), ()))
    width_share = lax.all_to_all(hidden, "dp", split_axis=1, concat_axis=0, tiled=True)
    grads_across = lax.all_gather(kv_grads, "dp", axis=0, tiled=True)
    gradients = lax.psum_scatter(
        lax.dot_general(
            width_share, grads_across, contract, preferred_element_type=jnp.float32
        ).astype(jnp.bfloat16),
        "ctx",
        scatter_dimension=0,
        tiled=True,
    ).astype(jnp.float32)
    kv_width = kv_heads * HD
    return (query_grad, key_grad, value_grad, gradients[:, :kv_width], gradients[:, kv_width:])


def solution(mesh):
    return jax.shard_map(
        on_device,
        mesh=mesh,
        in_specs=(
            P(("dp", "ctx"), None),
            P(("dp", "ctx"), None),
            P(("dp", "ctx"), None),
            P(("dp", "ctx"), None),
            P(("dp", "ctx"), None),
        ),
        out_specs=(
            P(("dp", "ctx"), None),
            P(("dp", "ctx"), None),
            P(("dp", "ctx"), None),
            P(("dp", "ctx"), None),
            P(("dp", "ctx"), None),
        ),
        check_vma=False,
    )
```

profile of v0, /device:TPU:1, one launch (start us, length us, event | category | flops | bytes accessed | tf_op | source)
XLA Modules:
  0.0 489.0 jit_solution(17524834126275159698)
XLA Ops:
  8.7 2.8 copy.408
  11.5 9.3 %all-to-all-start = ((bf16[192,16,256]{2,0,1:T(8,128)(2,1)}), bf16[192,16,256]{2,0,1:T(8,128)(2,1)S(1)}, u32[]{:S(2)}, u32[]{:S(2)}) async-start(bf16[192,16,256]{2,0,1:T(8,128)(2,1)} %bitcast.378), calls=%async_computation | async-start | bytes 3145728 | tf_op jit(solution)/shard_map/all_to_all | solution.py:19
  20.8 1.3 copy.407
  24.1 1.5 iota_compare_fusion.3
  25.6 1.8 iota_compare_fusion.2
  27.4 18.3 %all-to-all-done = bf16[192,16,256]{2,0,1:T(8,128)(2,1)S(1)} async-done(((bf16[192,16,256]{2,0,1:T(8,128)(2,1)}), bf16[192,16,256]{2,0,1:T(8,128)(2,1)S(1)}, u32[]{:S(2)}, u32[]{:S(2)}) %all-to-all-start) | async-done | bytes 1572896 | tf_op jit(solution)/shard_map/all_to_all | solution.py:19
  45.7 4.4 all-to-all-start.1
  50.2 2.2 iota_compare_fusion.1
  52.3 2.4 iota_compare_fusion
  54.8 1.8 reshape.425
  56.6 24.9 %all-to-all-done.1 = bf16[192,16,256]{2,0,1:T(8,128)(2,1)S(1)} async-done(((bf16[192,16,256]{2,0,1:T(8,128)(2,1)}), bf16[192,16,256]{2,0,1:T(8,128)(2,1)S(1)}, u32[]{:S(2)}, u32[]{:S(2)}) %all-to-all-start.1) | async-done | bytes 1572896 | tf_op jit(solution)/shard_map/all_to_all | solution.py:20
  82.2 3.3 fusion.227
  85.5 2.0 fusion.226
  87.6 2.0 fusion.229
  91.0 43.6 %all-gather.6.cloned.1.call-done = bf16[3072,512]{1,0:T(8,128)(2,1)} async-done(((bf16[192,512]{1,0:T(8,128)(2,1)}), bf16[3072,512]{1,0:T(8,128)(2,1)}) %all-gather.6.cloned.1.call-update) | async-done | bytes 3145744 | tf_op jit(solution)/shard_map/all_gather | solution.py:26
  134.5 1.6 fusion.82
  136.1 1.5 fusion.58
  139.6 4.8 fusion.232
  144.3 4.1 fusion.63
  148.5 6.5 %fusion.237 = (f32[2,512]{1,0:T(2,128)S(1)}, f32[2,512,1536]{1,2,0:T(8,128)}) fusion(pred[512,1536]{0,1:T(8,128)(4,1)} %iota_compare_fusion.3, bf16[3072,512]{1,0:T(8,128)(2,1)} %all-gather.4.cloned.1.call-done, s32[]{:T(128)S(6)} %select_n.34, bf16[512,2,128]{2,1,0:T(2,128)(2,1)} %get-tuple-element.199), kind=kOutput, calls=%fused_computation.274 | convolution fusion | flops 408946176 | bytes 7737348 | tf_op jit(solution)/shard_map/sub | solution.py:51
  155.0 5.3 %fusion.46 = bf16[2,512,1536]{1,2,0:T(8,128)(2,1)} fusion(f32[2,512,1536]{1,2,0:T(8,128)} %get-tuple-element.209, f32[2,512]{1,0:T(2,128)S(1)} %get-tuple-element.208), kind=kLoop, calls=%fused_computation.74 | loop fusion | flops 3145728 | bytes 9441280 | tf_op jit(solution)/shard_map/convert_element_type | solution.py:53
  160.3 8.5 %fusion.240 = (f32[2,512]{1,0:T(2,128)S(1)}, f32[2,512,2048]{1,2,0:T(8,128)}) fusion(pred[512,2048]{0,1:T(8,128)(4,1)} %iota_compare_fusion.2, bf16[3072,512]{1,0:T(8,128)(2,1)} %all-gather.4.cloned.1.call-done, s32[]{:T(128)S(6)} %select_n.34, bf16[512,2,128]{2,1,0:T(2,128)(2,1)} %get-tuple-element.198), kind=kOutput, calls=%fused_computation.275 | convolution fusion | flops 545261568 | bytes 10227716 | tf_op jit(solution)/shard_map/sub | solution.py:51
  168.8 6.5 %fusion.41 = bf16[2,512,2048]{1,2,0:T(8,128)(2,1)} fusion(f32[2,512,2048]{1,2,0:T(8,128)} %get-tuple-element.211, f32[2,512]{1,0:T(2,128)S(1)} %get-tuple-element.210), kind=kLoop, calls=%fused_computation.66 | loop fusion | flops 4194304 | bytes 12587008 | tf_op jit(solution)/shard_map/convert_element_type | solution.py:53
  175.3 9.5 %fusion.245 = (f32[2,512]{1,0:T(2,128)S(1)}, f32[2,512,2560]{1,2,0:T(8,128)}) fusion(pred[512,2560]{0,1:T(8,128)(4,1)} %iota_compare_fusion.1, bf16[3072,512]{1,0:T(8,128)(2,1)} %all-gather.4.cloned.1.call-done, s32[]{:T(128)S(6)} %select_n.34, bf16[512,2,128]{2,1,0:T(2,128)(2,1)} %get-tuple-element.197), kind=kOutput, calls=%fused_computation.276 | convolution fusion | flops 681576960 | bytes 12718084 | tf_op jit(solution)/shard_map/sub | solution.py:51
  184.8 7.8 %fusion.25 = bf16[2,512,2560]{1,2,0:T(8,128)(2,1)} fusion(f32[2,512,2560]{1,2,0:T(8,128)} %get-tuple-element.213, f32[2,512]{1,0:T(2,128)S(1)} %get-tuple-element.212), kind=kLoop, calls=%fused_computation.41 | loop fusion | flops 5242880 | bytes 15732736 | tf_op jit(solution)/shard_map/convert_element_type | solution.py:53
  192.5 11.2 %fusion.248 = (f32[2,512]{1,0:T(2,128)S(1)}, f32[2,512,3072]{1,2,0:T(8,128)}) fusion(pred[512,3072]{0,1:T(8,128)(4,1)} %iota_compare_fusion, bf16[3072,512]{1,0:T(8,128)(2,1)} %all-gather.4.cloned.1.call-done, s32[]{:T(128)S(6)} %select_n.34, bf16[512,2,128]{2,1,0:T(2,128)(2,1)} %get-tuple-element.196), kind=kOutput, calls=%fused_computation.277 | convolution fusion | flops 817892352 | bytes 15208452 | tf_op jit(solution)/shard_map/sub | solution.py:51
  203.7 9.1 %fusion.24 = bf16[2,512,3072]{1,2,0:T(8,128)(2,1)} fusion(f32[2,512,3072]{1,2,0:T(8,128)} %get-tuple-element.215, f32[2,512]{1,0:T(2,128)S(1)} %get-tuple-element.214), kind=kLoop, calls=%fused_computation.40 | loop fusion | flops 6291456 | bytes 18878464 | tf_op jit(solution)/shard_map/convert_element_type | solution.py:53
  212.9 2.5 fusion.70
  217.6 1.3 fusion.56
  218.9 1.6 fusion.37
  220.7 2.7 fusion.39
  223.4 4.6 all-to-all-start.4
  228.1 2.7 fusion.78
  230.8 3.1 fusion.27
  235.3 1.3 copy-done.9
  240.5 2.0 copy-done.5
  242.6 1.4 fusion.80
  244.0 1.3 fusion.12
  245.6 1.3 fusion.49
  248.1 1.6 fusion.77
  249.8 2.3 fusion.81
  252.1 5.1 %fusion.9 = bf16[2,512,2560]{1,2,0:T(8,128)(2,1)S(1)} fusion(f32[2,512]{1,0:T(2,128)S(1)} %fusion.77, f32[2,512,2560]{1,2,0:T(8,128)} %get-tuple-element.213, f32[2,512]{1,0:T(2,128)S(1)} %get-tuple-element.212, bf16[3072,512]{1,0:T(8,128)(2,1)S(1)} %copy-done.35, s32[]{:T(128)S(6)} %select_n.34, bf16[512,2,128]{2,1,0:T(2,128)(2,1)S(1)} %copy-done.20), kind=kOutput, calls=%fused_computation.13 | convolution fusion | flops 681574400 | bytes 16654340 | tf_op jit(solution)/shard_map/qhd,kd->hqk/dot_general | solution.py:59
  257.3 7.7 %fusion.7 = bf16[2,512,3072]{1,2,0:T(8,128)(2,1)S(1)} fusion(f32[2,512]{1,0:T(2,128)S(1)} %fusion.81, f32[2,512,3072]{1,2,0:T(8,128)} %get-tuple-element.215, f32[2,512]{1,0:T(2,128)S(1)} %get-tuple-element.214, bf16[3072,512]{1,0:T(8,128)(2,1)S(1)} %copy-done.35, s32[]{:T(128)S(6)} %select_n.34, bf16[512,2,128]{2,1,0:T(2,128)(2,1)S(1)} %copy-done.17), kind=kOutput, calls=%fused_computation.8 | convolution fusion | flops 817889280 | bytes 19931140 | tf_op jit(solution)/shard_map/qhd,kd->hqk/dot_general | solution.py:59
  265.0 1.7 fusion.35
  267.7 2.8 fusion.40
  270.4 7.6 %all-to-all-start.3 = ((bf16[16,192,128]{2,1,0:T(8,128)(2,1)}), bf16[16,192,128]{2,1,0:T(8,128)(2,1)}, u32[]{:S(2)}, u32[]{:S(2)}) async-start(bf16[16,192,128]{2,1,0:T(8,128)(2,1)} %bitcast.57), calls=%async_computation.3 | async-start | bytes 1572864 | tf_op jit(solution)/shard_map/all_to_all | solution.py:78
  278.1 1.2 bitcast_reduce_fusion
  279.4 13.2 %all-to-all-done.3 = bf16[16,192,128]{2,1,0:T(8,128)(2,1)} async-done(((bf16[16,192,128]{2,1,0:T(8,128)(2,1)}), bf16[16,192,128]{2,1,0:T(8,128)(2,1)}, u32[]{:S(2)}, u32[]{:S(2)}) %all-to-all-start.3) | async-done | bytes 786464 | tf_op jit(solution)/shard_map/all_to_all | solution.py:78
  294.7 2.1 copy.406
  296.8 4.6 all-to-all-start.5
  301.5 1.9 fusion.91
  303.5 69.7 %all-to-all-done.5 = bf16[192,8,1024]{2,0,1:T(8,128)(2,1)} async-done(((bf16[192,8,1024]{2,0,1:T(8,128)(2,1)}), bf16[192,8,1024]{2,0,1:T(8,128)(2,1)}, u32[]{:S(2)}, u32[]{:S(2)}) %all-to-all-start.5) | async-done | bytes 3145760 | tf_op jit(solution)/shard_map/all_to_all | solution.py:96
  373.2 23.8 %all-gather.8.cloned.1.call-done = bf16[1536,1024]{1,0:T(8,128)(2,1)} async-done(((bf16[192,1024]{1,0:T(8,128)(2,1)}), bf16[1536,1024]{1,0:T(8,128)(2,1)}) %all-gather.8.cloned.1.call-update) | async-done | bytes 3145744 | tf_op jit(solution)/shard_map/all_gather | solution.py:97
  397.0 6.3 %convert_bitcast_fusion = bf16[1024,1024]{0,1:T(8,128)(2,1)S(1)} fusion(bf16[1536,1024]{1,0:T(8,128)(2,1)} %all-gather.8.cloned.1.call-done, bf16[1536,1024]{1,0:T(8,128)(2,1)} %bitcast.70), kind=kOutput, calls=%fused_computation.93 | convolution fusion | flops 3222274048 | bytes 8388608 | tf_op jit(solution)/shard_map/dot_general | solution.py:99
  403.4 2.7 copy.281
  406.1 3.0 fusion.86
  409.2 2.5 fusion.95
  411.6 2.7 fusion.84
  414.3 4.5 fusion.88
  418.8 2.9 fusion.93
  421.7 3.6 copy.232
  426.3 33.6 %all_to_all.102 = bf16[16,192,256]{2,1,0:T(8,128)(2,1)S(1)} all-to-all(bf16[16,192,256]{2,1,0:T(8,128)(2,1)S(1)} %all_to_all.82), channel_id=1, replica_groups=mesh['dp'=8,'ctx'=16] {'ctx'}, dimensions={0} | all-to-all | bytes 3145728 | tf_op jit(solution)/shard_map/all_to_all | solution.py:76
  459.9 1.3 copy.298
  461.2 18.3 %reduce-scatter.4.cloned.1.call-done = bf16[64,1024]{1,0:T(8,128)(2,1)} async-done(((bf16[1024,1024]{1,0:T(8,128)(2,1)}), bf16[64,1024]{1,0:T(8,128)(2,1)}) %reduce-scatter.4.cloned.1.call-update) | async-done | bytes 131088
  (142 shorter events, 23.5 us)
Async XLA Ops:
  7.2 80.4 %all-gather.4.cloned.1.call-start = ((), (), s32[]{:S(2)}) async-start(), calls=%async_computation.7 | async-start | bytes 3342336 | tf_op jit(solution)/shard_map/all_gather | solution.py:25
  7.9 126.6 %all-gather.6.cloned.1.call-start = ((), (), s32[]{:S(2)}) async-start(), calls=%async_computation.8 | async-start | bytes 3342336 | tf_op jit(solution)/shard_map/all_gather | solution.py:26
  8.6 12.1 %copy-start.14 = (bf16[192,4096]{1,0:T(8,128)(2,1)S(1)}, bf16[192,4096]{1,0:T(8,128)(2,1)}, u32[]{:S(2)}) copy-start(bf16[192,4096]{1,0:T(8,128)(2,1)} %param.36) | copy-start | bytes 4718596
  11.5 34.3 %all-to-all-start = ((bf16[192,16,256]{2,0,1:T(8,128)(2,1)}), bf16[192,16,256]{2,0,1:T(8,128)(2,1)S(1)}, u32[]{:S(2)}, u32[]{:S(2)}) async-start(bf16[192,16,256]{2,0,1:T(8,128)(2,1)} %bitcast.378), calls=%async_computation | async-start | bytes 3145728 | tf_op jit(solution)/shard_map/all_to_all | solution.py:19
  45.7 35.8 %all-to-all-start.1 = ((bf16[192,16,256]{2,0,1:T(8,128)(2,1)}), bf16[192,16,256]{2,0,1:T(8,128)(2,1)S(1)}, u32[]{:S(2)}, u32[]{:S(2)}) async-start(bf16[192,16,256]{2,0,1:T(8,128)(2,1)} %bitcast.377), calls=%async_computation.1 | async-start | bytes 3145728 | tf_op jit(solution)/shard_map/all_to_all | solution.py:20
  85.5 4.0 copy-start.27
  89.6 1.0 copy-start.29
  136.1 1.5 copy-start.28
  137.6 1.0 copy-start.10
  138.6 0.7 copy-start.30
  203.7 11.6 %copy-start.8 = (bf16[2,512,1536]{1,2,0:T(8,128)(2,1)S(1)}, bf16[2,512,1536]{1,2,0:T(8,128)(2,1)}, u32[]{:S(2)}) copy-start(bf16[2,512,1536]{1,2,0:T(8,128)(2,1)} %fusion.46) | copy-start | bytes 9437188
  212.9 2.5 copy-start.24
  212.9 6.0 %slice-start.6 = ((s8[5242880]{0:T(1024)(128)(4,1)}), s8[4194304]{0:T(1024)(128)(4,1)S(1)}, s32[]{:S(2)}) async-start(s8[5242880]{0:T(1024)(128)(4,1)} %bitcast.385), calls=%async_computation.17 | async-start | bytes 8388608
  215.4 2.2 copy-start.4
  215.4 2.2 copy-start.22
  215.4 3.5 slice-start.7
  217.6 1.3 copy-start.19
  217.6 2.9 slice-start.2
  218.9 1.8 slice-start.3
  218.9 1.8 copy-start.17
  223.4 7.3 %copy-start.26 = (bf16[512,2,128]{2,1,0:T(2,128)(2,1)S(1)}, bf16[512,2,128]{2,1,0:T(2,128)(2,1)}, u32[]{:S(2)}) copy-start(bf16[512,2,128]{2,1,0:T(2,128)(2,1)} %get-tuple-element.194) | copy-start | bytes 786436
  223.4 47.0 %all-to-all-start.4 = ((bf16[16,192,128]{2,1,0:T(8,128)(2,1)}), bf16[16,192,128]{2,1,0:T(8,128)(2,1)}, u32[]{:S(2)}, u32[]{:S(2)}) async-start(bf16[16,192,128]{2,1,0:T(8,128)(2,1)} %bitcast.396), calls=%async_computation.4 | async-start | bytes 1572864 | tf_op jit(solution)/shard_map/all_to_all | solution.py:81
  228.0 9.8 %slice-start.12 = ((s8[6291456]{0:T(1024)(128)(4,1)}), s8[4194304]{0:T(1024)(128)(4,1)S(1)}, s32[]{:S(2)}) async-start(s8[6291456]{0:T(1024)(128)(4,1)} %bitcast.394), calls=%async_computation.23 | async-start | bytes 8388608
  230.7 3.2 copy-start.31
  230.7 3.2 copy-start.34
  230.8 4.6 copy-start.25
  230.8 4.6 copy-start.35
  230.8 7.0 %slice-start.13 = ((s8[6291456]{0:T(1024)(128)(4,1)}), s8[2097152]{0:T(1024)(128)(4,1)S(1)}, s32[]{:S(2)}) async-start(s8[6291456]{0:T(1024)(128)(4,1)} %bitcast.394), calls=%async_computation.24 | async-start | bytes 4194304
  234.0 1.4 copy-start.13
  234.0 2.7 copy-start.9
  236.7 7.3 %slice-start.10 = ((s8[8388608]{0:T(1024)(128)(4,1)}), s8[4194304]{0:T(1024)(128)(4,1)S(1)}, s32[]{:S(2)}) async-start(s8[8388608]{0:T(1024)(128)(4,1)} %bitcast.389), calls=%async_computation.21 | async-start | bytes 8388608
  237.8 1.1 copy-start.21
  237.8 6.1 %slice-start.11 = ((s8[8388608]{0:T(1024)(128)(4,1)}), s8[4194304]{0:T(1024)(128)(4,1)S(1)}, s32[]{:S(2)}) async-start(s8[8388608]{0:T(1024)(128)(4,1)} %bitcast.389), calls=%async_computation.22 | async-start | bytes 8388608
  238.9 1.6 copy-start.6
  238.9 3.6 copy-start.5
  238.9 3.7 copy-start.23
  242.6 5.1 %slice-start.8 = ((s8[5242880]{0:T(1024)(128)(4,1)}), s8[4194304]{0:T(1024)(128)(4,1)S(1)}, s32[]{:S(2)}) async-start(s8[5242880]{0:T(1024)(128)(4,1)} %bitcast.387), calls=%async_computation.19 | async-start | bytes 8388608
  242.6 7.2 %slice-start.4 = ((s8[6291456]{0:T(1024)(128)(4,1)}), s8[4194304]{0:T(1024)(128)(4,1)S(1)}, s32[]{:S(2)}) async-start(s8[6291456]{0:T(1024)(128)(4,1)} %bitcast.383), calls=%async_computation.15 | async-start | bytes 8388608
  244.0 1.6 copy-start.18
  244.0 3.7 slice-start.9
  244.0 5.8 %slice-start.5 = ((s8[6291456]{0:T(1024)(128)(4,1)}), s8[2097152]{0:T(1024)(128)(4,1)S(1)}, s32[]{:S(2)}) async-start(s8[6291456]{0:T(1024)(128)(4,1)} %bitcast.383), calls=%async_computation.16 | async-start | bytes 4194304
  245.6 2.1 copy-start.2
  245.6 2.5 copy-start.20
  257.2 7.8 %copy-start.1 = (bf16[2,512,2560]{1,2,0:T(8,128)(2,1)}, bf16[2,512,2560]{1,2,0:T(8,128)(2,1)S(1)}, u32[]{:S(2)}) copy-start(bf16[2,512,2560]{1,2,0:T(8,128)(2,1)S(1)} %fusion.9) | copy-start | bytes 15728644
  257.2 7.8 %copy-start.16 = (bf16[512,2,128]{2,1,0:T(2,128)(2,1)S(1)}, bf16[512,2,128]{2,1,0:T(2,128)(2,1)}, u32[]{:S(2)}) copy-start(bf16[512,2,128]{2,1,0:T(2,128)(2,1)} %get-tuple-element.197) | copy-start | bytes 786436
  265.0 2.6 copy-start
  265.0 2.6 copy-start.15
  270.4 24.3 %copy-start.12 = (bf16[192,8192]{1,0:T(8,128)(2,1)S(1)}, bf16[192,8192]{1,0:T(8,128)(2,1)}, u32[]{:S(2)}) copy-start(bf16[192,8192]{1,0:T(8,128)(2,1)} %param.37) | copy-start | bytes 9437188
  270.4 22.1 %all-to-all-start.3 = ((bf16[16,192,128]{2,1,0:T(8,128)(2,1)}), bf16[16,192,128]{2,1,0:T(8,128)(2,1)}, u32[]{:S(2)}, u32[]{:S(2)}) async-start(bf16[16,192,128]{2,1,0:T(8,128)(2,1)} %bitcast.57), calls=%async_computation.3 | async-start | bytes 1572864 | tf_op jit(solution)/shard_map/all_to_all | solution.py:78
  278.0 119.0 %all-gather.8.cloned.1.call-start = ((), (), s32[]{:S(2)}) async-start(), calls=%async_computation.9 | async-start | bytes 3538944 | tf_op jit(solution)/shard_map/all_gather | solution.py:97
  279.4 17.4 %copy-start.32 = (bf16[192,512]{1,0:T(8,128)(2,1)}, bf16[192,512]{1,0:T(8,128)(2,1)S(1)}, u32[]{:S(2)}) copy-start(bf16[192,512]{1,0:T(8,128)(2,1)S(1)} %copy_bitcast_fusion.3) | copy-start | bytes 589828
  293.8 3.0 copy-start.33
  296.8 4.7 copy-start.11
  296.8 76.4 %all-to-all-start.5 = ((bf16[192,8,1024]{2,0,1:T(8,128)(2,1)}), bf16[192,8,1024]{2,0,1:T(8,128)(2,1)}, u32[]{:S(2)}, u32[]{:S(2)}) async-start(bf16[192,8,1024]{2,0,1:T(8,128)(2,1)} %bitcast.376), calls=%async_computation.5 | async-start | bytes 6291456 | tf_op jit(solution)/shard_map/all_to_all | solution.py:96
  301.5 178.1 %reduce-scatter.4.cloned.1.call-start = ((), (), s32[]{:S(2)}) async-start(), calls=%async_computation.10 | async-start | bytes 2228224
  406.1 3.1 copy-start.7
  406.1 5.5 %copy-start.3 = (bf16[2,512,2048]{1,2,0:T(8,128)(2,1)S(1)}, bf16[2,512,2048]{1,2,0:T(8,128)(2,1)}, u32[]{:S(2)}) copy-start(bf16[2,512,2048]{1,2,0:T(8,128)(2,1)} %copy-done.2) | copy-start | bytes 12582916
  409.2 9.6 %slice-start = ((s8[6291456]{0:T(1024)(128)(4,1)}), s8[4194304]{0:T(1024)(128)(4,1)S(1)}, s32[]{:S(2)}) async-start(s8[6291456]{0:T(1024)(128)(4,1)} %bitcast.379), calls=%async_computation.11 | async-start | bytes 8388608
  411.6 7.1 %slice-start.1 = ((s8[6291456]{0:T(1024)(128)(4,1)}), s8[2097152]{0:T(1024)(128)(4,1)S(1)}, s32[]{:S(2)}) async-start(s8[6291456]{0:T(1024)(128)(4,1)} %bitcast.379), calls=%async_computation.12 | async-start | bytes 4194304
Sparse Core Ops, SparseCore 0:
  10.5 71.2 all-gather.3
  84.2 50.2 all-gather.5
  294.8 102.1 all-gather.7
  406.3 73.2 reduce-scatter.3
where the time goes:
time: 496 us; the launch traced here: 489 us
  waiting for transfers between devices  213 us (43%)
  matrix products  114 us (23%)
  other arithmetic  46.3 us (9%)
  local copies, waits for them, and re-layouts  36.4 us (7%)
  blocking collectives  33.6 us (7%)
  starting transfers between devices  30.7 us (6%)
  between operations  14.6 us (3%)
    all_to_all x1, waiting for transfers between devices, on_device(): lax.all_to_all(hidden, 'dp', split_axis=1, concat_axis=0, tiled=True)  69.7 us
    all_gather x1, waiting for transfers between devices, on_device(): lax.all_gather(values, 'ctx', axis=0, tiled=True)  43.6 us
    sub x6, matrix products, on_device(): exponent = jnp.exp(scores - row_max)  42.4 us
    all_to_all x1, blocking collectives, on_device(): lax.all_to_all(query_local, 'ctx', split_axis=0, concat_axis=1, tiled=True)  33.6 us
    convert_element_type x6, other arithmetic, on_device(): prob_low = probability.astype(jnp.bfloat16)  33.1 us
    all_to_all x1, waiting for transfers between devices, on_device(): lax.all_to_all(out_grad, 'ctx', split_axis=1, concat_axis=0, tiled=True)  24.9 us
    all_gather x1, waiting for transfers between devices, on_device(): grads_across = lax.all_gather(kv_grads, 'dp', axis=0, tiled=True)  23.8 us
    unnamed x5, waiting for transfers between devices  19.8 us
  transfers between devices with their start and end apart: 9, of which 7 were waited for; matrix products, arithmetic and copies ran while one was open for 17% of the time, Pallas kernels for 0%

commit v1 on v0

v1 whole, which is shorter than its diff:
```python
import functools
import math

import jax
import jax.numpy as jnp
from jax import lax
from jax.experimental import pallas as pl
from jax.experimental.pallas import tpu as pltpu
from jax.sharding import PartitionSpec as P

MESH = pl.DeviceIdType.MESH
HD = 128
NZ, NX, NC = 4, 2, 2
NB = NZ * NX
LANES = 768
SCALE = 1.0 / math.sqrt(HD)
SCALE2 = SCALE * math.log2(math.e)
F32, BF16 = jnp.float32, jnp.bfloat16


def dot(a, b, ca=1, cb=0):
    return lax.dot_general(a, b, (((ca,), (cb,)), ((), ())), preferred_element_type=F32)


def kernel(
    n_dp,
    q_in,
    k_in,
    v_in,
    g_in,
    h_in,
    dq_out,
    dk_out,
    dv_out,
    wk_out,
    wv_out,
    q_buf,
    g_buf,
    kv_buf,
    q_t,
    g_t,
    e_buf,
    p_buf,
    m_buf,
    acc,
    dq_buf,
    core_send,
    core_recv,
    x_send,
    x_recv,
    fin,
    h_buf,
    kvg,
    w_part,
    wc_send,
    wc_recv,
    w_send,
    w_recv,
    w_k,
    w_v,
    s_q,
    s_g,
    s_kv,
    s_fw,
    s_h,
    s_dq,
    s_misc,
    r_q,
    r_g,
    r_kv,
    r_fw,
    r_h,
    r_dq,
    r_core,
    r_x,
    r_fin,
    r_kvg,
    r_wc,
    r_w,
    o_sem,
):
    me_dp = lax.axis_index("dp")
    me = lax.axis_index("ctx")
    z, x, c = me // (NX * NC), (me // NC) % NX, me % NC
    oc = 1 - c
    tok = q_in.shape[0]
    blk = tok * NC
    heads = q_in.shape[1] // HD
    per_dev = heads // (NZ * NC)
    kv_cols = k_in.shape[1]
    rows = per_dev * blk

    def ctx_dev(zz, xx, cc):
        return (me_dp, (zz * NX + xx) * NC + cc)

    def remote(src, dst, ssem, rsem, dev):
        return pltpu.make_async_remote_copy(
            src_ref=src, dst_ref=dst, send_sem=ssem, recv_sem=rsem, device_id=dev, device_id_type=MESH
        )

    def wait_bytes(ref, sem):
        pltpu.make_async_copy(ref, ref, sem).wait()

    barrier = pltpu.get_barrier_semaphore()
    n_ctx = NZ * NX * NC
    for d in range(1, n_ctx):
        pl.semaphore_signal(barrier, inc=1, device_id=(me_dp, lax.rem(me + d, n_ctx)), device_id_type=MESH)
    for d in range(1, n_dp):
        pl.semaphore_signal(barrier, inc=1, device_id=(lax.rem(me_dp + d, n_dp), me), device_id_type=MESH)
    pl.semaphore_wait(barrier, n_ctx - 1 + n_dp - 1)

    my_block = z * NX + x
    for dz in range(NZ):
        gz = lax.rem(z + dz, NZ)
        cols = pl.ds(pl.multiple_of(gz * HD, HD), HD)
        for dx in range(NX):
            gx = lax.rem(x + dx, NX)
            for which, src in ((0, k_in), (1, v_in)):
                dst = kv_buf.at[my_block, c, which]
                if dz == 0 and dx == 0:
                    pltpu.make_async_copy(src.at[:, cols], dst, r_kv.at[my_block]).start()
                else:
                    remote(src.at[:, cols], dst, s_kv, r_kv.at[my_block], ctx_dev(gz, gx, c)).start()
    for dz in range(NZ):
        gz = lax.rem(z + dz, NZ)
        for dc in range(NC):
            gc = lax.rem(c + dc, NC)
            for a in range(per_dev):
                col = ((gz * NC + gc) * per_dev + a) * HD
                cols = pl.ds(pl.multiple_of(col, HD), HD)
                spot = pl.ds(pl.multiple_of(c * tok, tok), tok)
                for src, buf, ssem, rsem in ((q_in, q_buf, s_q, r_q), (g_in, g_buf, s_g, r_g)):
                    dst = buf.at[z, a, spot, :]
                    if dz == 0 and dc == 0:
                        pltpu.make_async_copy(src.at[:, cols], dst, rsem.at[z]).start()
                    else:
                        remote(src.at[:, cols], dst, ssem, rsem.at[z], ctx_dev(gz, x, gc)).start()
    share = h_in.shape[1] // n_dp
    for d in range(n_dp):
        gd = lax.rem(me_dp + d, n_dp)
        cols = pl.ds(pl.multiple_of(gd * share, HD), share)
        if d == 0:
            pltpu.make_async_copy(h_in.at[:, cols], h_buf.at[me_dp], r_h).start()
        else:
            remote(h_in.at[:, cols], h_buf.at[me_dp], s_h, r_h, (gd, me)).start()

    acc[...] = jnp.zeros_like(acc)
    for d in range(NB):
        b = lax.rem(my_block + d, NB)
        wait_bytes(kv_buf.at[b, c], r_kv.at[b])
        remote(kv_buf.at[b, c], kv_buf.at[b, c], s_fw.at[b], r_fw.at[b], ctx_dev(z, x, oc)).start()
    for d in range(NB):
        b = lax.rem(my_block + d, NB)
        wait_bytes(kv_buf.at[b, oc], r_fw.at[b])

    def attend(step, carry):
        later = NZ - step
        zq = jnp.where(step == 0, z, jnp.where(later <= z, later - 1, later))
        last = zq * NX + x
        wait_bytes(q_buf.at[zq], r_q.at[zq])
        wait_bytes(g_buf.at[zq], r_g.at[zq])
        for a in range(per_dev):
            q_t[:, a * blk : (a + 1) * blk] = q_buf[zq, a].T
            g_t[:, a * blk : (a + 1) * blk] = g_buf[zq, a].T
        heads_in = LANES // blk
        for part in range(rows // LANES):
            lanes = slice(part * LANES, (part + 1) * LANES)
            qt, gt = q_t[:, lanes], g_t[:, lanes]
            hs = pl.ds(part * heads_in, heads_in)

            def first(b, carry, masked):
                top, total, delta = carry
                at = pl.ds(pl.multiple_of(b * blk, blk), blk)
                kb = kv_buf[b, :, 0].reshape(blk, HD)
                vb = kv_buf[b, :, 1].reshape(blk, HD)
                s = dot(kb, qt) * SCALE2
                if masked:
                    key_id = lax.broadcasted_iota(jnp.int32, (blk, blk), 0)
                    query_id = lax.broadcasted_iota(jnp.int32, (blk, blk), 1)
                    seen = key_id <= query_id
                    s = jnp.concatenate(
                        [jnp.where(seen, s[:, i * blk : (i + 1) * blk], -jnp.inf) for i in range(heads_in)], 1
                    )
                dp = dot(vb, gt)
                new = jnp.maximum(top, jnp.max(s, axis=0, keepdims=True))
                shrink = jnp.exp2(top - new)
                e = jnp.exp2(s - new)
                total = total * shrink + jnp.sum(e, axis=0, keepdims=True)
                delta = delta * shrink + jnp.sum(e * dp, axis=0, keepdims=True)
                e_buf[at, :] = e
                p_buf[at, :] = dp
                m_buf[pl.ds(b, 1), :] = new
                return new, total, delta

            zero = jnp.zeros((1, LANES), F32)
            stats = lax.fori_loop(0, last, lambda b, t: first(b, t, False), (zero - jnp.inf, zero, zero))
            top, total, delta = first(last, stats, True)
            inv = 1.0 / total
            delta = delta * inv

            def second(b, dqt):
                at = pl.ds(pl.multiple_of(b * blk, blk), blk)
                fix = jnp.exp2(m_buf[pl.ds(b, 1), :] - top) * inv
                prob = e_buf[at, :] * fix
                low = prob.astype(BF16)
                ds = (prob * (p_buf[at, :] - delta)).astype(BF16)
                kb = kv_buf[b, :, 0].reshape(blk, HD)
                gh = g_buf[zq, hs].reshape(LANES, HD)
                qh = q_buf[zq, hs].reshape(LANES, HD)
                acc[0, b] += dot(ds, qh).reshape(NC, tok, HD)
                acc[1, b] += dot(low, gh).reshape(NC, tok, HD)
                return dqt + dot(kb.T, ds)

            dqt = lax.fori_loop(0, last + 1, second, jnp.zeros((HD, LANES), F32))
            for i in range(heads_in):
                head = dqt[:, i * blk : (i + 1) * blk] * SCALE
                dq_buf[zq, part * heads_in + i] = head.T.astype(BF16)
        for gc in range(NC):
            mine = jnp.logical_and(zq == z, c == gc)
            for a in range(per_dev):
                col = ((z * NC + c) * per_dev + a) * HD
                cols = pl.ds(pl.multiple_of(col, HD), HD)
                src = dq_buf.at[zq, a, gc * tok : (gc + 1) * tok, :]

                @pl.when(mine)
                def _():
                    pltpu.make_async_copy(src, dq_out.at[:, cols], r_dq).start()

                @pl.when(jnp.logical_not(mine))
                def _():
                    remote(src, dq_out.at[:, cols], s_dq, r_dq, ctx_dev(zq, x, gc)).start()

        return carry

    lax.fori_loop(0, NZ, attend, 0)

    for b in range(NB):
        core_send[b, 0] = (acc[0, b, oc] * SCALE).astype(BF16)
        core_send[b, 1] = acc[1, b, oc].astype(BF16)
    over_core = remote(core_send, core_recv, s_misc.at[0], r_core, ctx_dev(z, x, oc))
    over_core.start()
    over_core.wait()
    for zz in range(NZ):
        b = zz * NX + (1 - x)
        x_send[zz, 0] = (acc[0, b, c] * SCALE + core_recv[b, 0].astype(F32)).astype(BF16)
        x_send[zz, 1] = (acc[1, b, c] + core_recv[b, 1].astype(F32)).astype(BF16)
    over_x = remote(x_send, x_recv, s_misc.at[1], r_x, ctx_dev(z, 1 - x, c))
    over_x.start()
    over_x.wait()
    for zz in range(NZ):
        b = zz * NX + x
        fin[zz, 0] = (
            acc[0, b, c] * SCALE + core_recv[b, 0].astype(F32) + x_recv[zz, 0].astype(F32)
        ).astype(BF16)
        fin[zz, 1] = (acc[1, b, c] + core_recv[b, 1].astype(F32) + x_recv[zz, 1].astype(F32)).astype(BF16)
    for dz in range(NZ):
        gz = lax.rem(z + dz, NZ)
        for which in range(2):
            cols = pl.ds(pl.multiple_of(which * kv_cols + z * HD, HD), HD)
            dst = kvg.at[me_dp, :, cols]
            if dz == 0:
                pltpu.make_async_copy(fin.at[gz, which], dst, r_fin).start()
            else:
                remote(fin.at[gz, which], dst, s_misc.at[2], r_fin, ctx_dev(gz, x, c)).start()
    wait_bytes(kvg.at[me_dp], r_fin)
    for d in range(1, n_dp):
        gd = lax.rem(me_dp + d, n_dp)
        remote(kvg.at[me_dp], kvg.at[me_dp], s_misc.at[3], r_kvg.at[me_dp], (gd, me)).start()
    out_k = pltpu.make_async_copy(kvg.at[me_dp, :, 0:kv_cols], dk_out, o_sem.at[0])
    out_v = pltpu.make_async_copy(kvg.at[me_dp, :, kv_cols : 2 * kv_cols], dv_out, o_sem.at[1])
    out_k.start()
    out_v.start()
    wait_bytes(h_buf, r_h)
    for d in range(1, n_dp):
        gd = lax.rem(me_dp + d, n_dp)
        wait_bytes(kvg.at[gd], r_kvg.at[gd])
    width = 2 * kv_cols
    grads = kvg[...].reshape(n_dp * tok, width)
    out_rows = w_part.shape[2]
    chunk = NX * NC * out_rows

    def project(zz, carry):
        cols = pl.ds(pl.multiple_of(zz * chunk, chunk), chunk)
        hid = h_buf[:, :, cols].reshape(n_dp * tok, chunk)
        res = dot(hid, grads, 0, 0)
        w_part[pl.ds(zz * NX, NX)] = res.reshape(NX, NC, out_rows, width)
        return carry

    lax.fori_loop(0, NZ, project, 0)
    for b in range(NB):
        wc_send[b] = w_part[b, oc].astype(BF16)
    over_core = remote(wc_send, wc_recv, s_misc.at[4], r_wc, ctx_dev(z, x, oc))
    over_core.start()
    over_core.wait()
    for b in range(NB):
        w_send[b] = (w_part[b, c] + wc_recv[b].astype(F32)).astype(BF16)
    for d in range(1, NB):
        b = lax.rem(my_block + d, NB)
        remote(
            w_send.at[b], w_recv.at[my_block], s_misc.at[5], r_w.at[my_block], ctx_dev(b // NX, lax.rem(b, NX), c)
        ).start()
    total = w_part[my_block, c] + wc_recv[my_block].astype(F32)
    for d in range(1, NB):
        b = lax.rem(my_block + d, NB)
        wait_bytes(w_recv.at[b], r_w.at[b])
        total = total + w_recv[b].astype(F32)
    w_k[...] = total[:, :kv_cols]
    w_v[...] = total[:, kv_cols:]
    out_wk = pltpu.make_async_copy(w_k, wk_out, o_sem.at[2])
    out_wv = pltpu.make_async_copy(w_v, wv_out, o_sem.at[3])
    out_wk.start()
    out_wv.start()

    wait_bytes(dq_out, r_dq)
    part = heads - per_dev
    wait_bytes(q_in.at[:, : part * HD], s_q)
    wait_bytes(g_in.at[:, : part * HD], s_g)
    wait_bytes(q_in.at[:, : part * HD], s_dq)
    wait_bytes(q_in.at[:, : (NB - 1) * 2 * HD], s_kv)
    for b in range(NB):
        wait_bytes(kv_buf.at[b, c], s_fw.at[b])
    wait_bytes(h_in.at[:, : (n_dp - 1) * share], s_h)
    wait_bytes(fin.at[pl.ds(0, NZ - 1)], s_misc.at[2])
    wait_bytes(kvg.at[pl.ds(0, n_dp - 1)], s_misc.at[3])
    wait_bytes(w_send.at[pl.ds(0, NB - 1)], s_misc.at[5])
    out_k.wait()
    out_v.wait()
    out_wk.wait()
    out_wv.wait()


def on_device(n_dp, queries, keys, values, out_grad, hidden):
    tok, width = queries.shape
    kv_cols = keys.shape[1]
    blk = tok * NC
    per_dev = width // HD // (NZ * NC)
    rows = per_dev * blk
    share = hidden.shape[1] // n_dp
    out_rows = share // (NZ * NX * NC)
    dma = pltpu.SemaphoreType.DMA
    any_spec = pl.BlockSpec(memory_space=pl.ANY)
    return pl.pallas_call(
        functools.partial(kernel, n_dp),
        out_shape=[
            jax.ShapeDtypeStruct(queries.shape, BF16),
            jax.ShapeDtypeStruct(keys.shape, BF16),
            jax.ShapeDtypeStruct(values.shape, BF16),
            jax.ShapeDtypeStruct((out_rows, kv_cols), F32),
            jax.ShapeDtypeStruct((out_rows, kv_cols), F32),
        ],
        in_specs=[any_spec] * 5,
        out_specs=[any_spec] * 5,
        scratch_shapes=[
            pltpu.VMEM((NZ, per_dev, blk, HD), BF16),
            pltpu.VMEM((NZ, per_dev, blk, HD), BF16),
            pltpu.VMEM((NB, NC, 2, tok, HD), BF16),
            pltpu.VMEM((HD, rows), BF16),
            pltpu.VMEM((HD, rows), BF16),
            pltpu.VMEM((NB * blk, LANES), F32),
            pltpu.VMEM((NB * blk, LANES), F32),
            pltpu.VMEM((NB, LANES), F32),
            pltpu.VMEM((2, NB, NC, tok, HD), F32),
            pltpu.VMEM((NZ, per_dev, blk, HD), BF16),
            pltpu.VMEM((NB, 2, tok, HD), BF16),
            pltpu.VMEM((NB, 2, tok, HD), BF16),
            pltpu.VMEM((NZ, 2, tok, HD), BF16),
            pltpu.VMEM((NZ, 2, tok, HD), BF16),
            pltpu.VMEM((NZ, 2, tok, HD), BF16),
            pltpu.VMEM((n_dp, tok, share), BF16),
            pltpu.VMEM((n_dp, tok, 2 * kv_cols), BF16),
            pltpu.VMEM((NB, NC, out_rows, 2 * kv_cols), F32),
            pltpu.VMEM((NB, out_rows, 2 * kv_cols), BF16),
            pltpu.VMEM((NB, out_rows, 2 * kv_cols), BF16),
            pltpu.VMEM((NB, out_rows, 2 * kv_cols), BF16),
            pltpu.VMEM((NB, out_rows, 2 * kv_cols), BF16),
            pltpu.VMEM((out_rows, kv_cols), F32),
            pltpu.VMEM((out_rows, kv_cols), F32),
            dma,
            dma,
            dma,
            dma((NB,)),
            dma,
            dma,
            dma((6,)),
            dma((NZ,)),
            dma((NZ,)),
            dma((NB,)),
            dma((NB,)),
            dma,
            dma,
            dma,
            dma,
            dma,
            dma((n_dp,)),
            dma,
            dma((NB,)),
            dma((4,)),
        ],
        compiler_params=pltpu.CompilerParams(
            collective_id=0, has_side_effects=True, vmem_limit_bytes=58 * 1024 * 1024
        ),
        cost_estimate=pl.CostEstimate(
            flops=40_000_000_000, bytes_accessed=20_000_000, transcendentals=10_000_000
        ),
        name="attention_backward",
    )(queries, keys, values, out_grad, hidden)


def solution(mesh):
    spec = P(("dp", "ctx"), None)
    return jax.shard_map(
        functools.partial(on_device, mesh.shape["dp"]),
        mesh=mesh,
        in_specs=(spec,) * 5,
        out_specs=(spec,) * 5,
        check_vma=False,
    )
```

time: 496 us -> 182 us (0.37); the launches traced: 489 us -> 181 us
  waiting for transfers between devices: 213 us -> 0 us
  Pallas kernels: 0 us -> 175 us
  matrix products: 114 us -> 0 us
  other arithmetic: 46.3 us -> 0 us
  blocking collectives: 33.6 us -> 0 us
  local copies, waits for them, and re-layouts: 36.4 us -> 5.45 us
  starting transfers between devices: 30.7 us -> 0 us
  between operations: 14.6 us -> 0.68 us
    pallas_call x0 -> x1, Pallas kernels: none -> 175 us  [on_device(): pl.pallas_call(functools.partial(kernel, n_dp), out_shape=[jax.ShapeDtype...]
    all_to_all x5 -> x0, waiting for transfers between devices: 126 us -> none  [the longest x1 69.7 us: on_device(): lax.all_to_all(hidden, 'dp', split_axis=1, concat_axis=0, tiled=True)]
    dot_general x31 -> x0, matrix products: 71.6 us -> none  [the longest x6 19.7 us: on_device(): jnp.einsum('qhd,kd->hqk', grad_block, value_block, preferred_element_type...]
    all_gather x3 -> x0, waiting for transfers between devices: 67.4 us -> none  [the longest x1 43.6 us: on_device(): lax.all_gather(values, 'ctx', axis=0, tiled=True)]
    sub x6 -> x0, matrix products: 42.4 us -> none  [on_device(): exponent = jnp.exp(scores - row_max)]
    all_to_all x1 -> x0, blocking collectives: 33.6 us -> none  [on_device(): lax.all_to_all(query_local, 'ctx', split_axis=0, concat_axis=1, tiled=True)]
    convert_element_type x6 -> x0, other arithmetic: 33.1 us -> none  [on_device(): prob_low = probability.astype(jnp.bfloat16)]
    all_to_all x5 -> x0, starting transfers between devices: 30.6 us -> none  [the longest x1 9.29 us: on_device(): lax.all_to_all(queries, 'ctx', split_axis=1, concat_axis=0, tiled=True)]
  transfers between devices with their start and end apart: 9 -> 0, of which waited for: 7 -> 0; matrix products, arithmetic and copies ran while one was open for 17% -> 0% of each run, Pallas kernels for 0% -> 0%
where the time goes in v1:
time: 182 us; the launch traced here: 181 us
  Pallas kernels  175 us (96%)
  local copies, waits for them, and re-layouts  5.45 us (3%)
    pallas_call x1, Pallas kernels, on_device(): pl.pallas_call(functools.partial(kernel, n_dp), out_shape=[jax.ShapeDtype...  175 us
    unnamed x13, local copies, waits for them, and re-layouts  5.45 us

profile of v1, /device:TPU:1, one launch (start us, length us, event | category | flops | bytes accessed | tf_op | source)
XLA Modules:
  0.0 181.5 jit_solution(10120923068574172228)
XLA Ops:
  0.6 175.3 %attention_backward.1 = (bf16[192,4096]{1,0:T(8,128)(2,1)}, bf16[192,512]{1,0:T(8,128)(2,1)}, bf16[192,512]{1,0:T(8,128)(2,1)}, f32[64,512]{1,0:T(8,128)}, f32[64,512]{1,0:T(8,128)}) custom-call(bf16[192,4096]{1,0:T(8,128)(2,1)} %q_in.1, bf16[192,512]{1,0:T(8,128)(2,1)} %k_in.1, bf16[192,512]{1,0:T(8,128)(2,1)} %v_in.1, bf16[192,4096]{1,0:T(8,128)(2,1)} %g_in.1, ...), custom_call_target="tpu_custom_call" | custom-call | flops 40000000000 | bytes 20000000 | tf_op jit(solution)/shard_map/attention_backward/pallas_call | solution.py:342
  176.0 0.0 copy-start.1
  176.0 0.0 copy-start
  176.0 0.0 copy-start.3
  176.0 0.0 copy-start.2
  176.0 2.8 %copy.15 = bf16[192,4096]{1,0:T(8,128)(2,1)} copy(bf16[192,4096]{1,0:T(8,128)(2,1)} %get-tuple-element.10) | data formatting | bytes 3145728
  178.8 0.0 copy-done.1
  178.8 0.7 copy.16
  179.5 0.0 copy-done
  179.5 0.7 copy.17
  180.1 0.0 copy-done.3
  180.1 0.7 copy.18
  180.8 0.0 copy-done.2
  180.8 0.7 copy.19
Async XLA Ops:
  176.0 2.8 %copy-start.1 = (bf16[192,512]{1,0:T(8,128)(2,1)S(1)}, bf16[192,512]{1,0:T(8,128)(2,1)}, u32[]{:S(2)}) copy-start(bf16[192,512]{1,0:T(8,128)(2,1)} %get-tuple-element.11) | copy-start | bytes 589828
  176.0 3.5 %copy-start = (bf16[192,512]{1,0:T(8,128)(2,1)S(1)}, bf16[192,512]{1,0:T(8,128)(2,1)}, u32[]{:S(2)}) copy-start(bf16[192,512]{1,0:T(8,128)(2,1)} %get-tuple-element.12) | copy-start | bytes 589828
  176.0 4.1 %copy-start.3 = (f32[64,512]{1,0:T(8,128)S(1)}, f32[64,512]{1,0:T(8,128)}, u32[]{:S(2)}) copy-start(f32[64,512]{1,0:T(8,128)} %get-tuple-element.13) | copy-start | bytes 393220
  176.0 4.8 %copy-start.2 = (f32[64,512]{1,0:T(8,128)S(1)}, f32[64,512]{1,0:T(8,128)}, u32[]{:S(2)}) copy-start(f32[64,512]{1,0:T(8,128)} %get-tuple-element.14) | copy-start | bytes 393220

commit v2 on v1

v2 whole, which is shorter than its diff:
```python
import functools
import math

import jax
import jax.numpy as jnp
from jax import lax
from jax.experimental import pallas as pl
from jax.experimental.pallas import tpu as pltpu
from jax.sharding import PartitionSpec as P

MESH = pl.DeviceIdType.MESH
HD = 128
NZ, NX, NC = 4, 2, 2
NB = NZ * NX
SCALE = 1.0 / math.sqrt(HD)
SCALE2 = SCALE * math.log2(math.e)
F32, BF16 = jnp.float32, jnp.bfloat16


def dot(a, b, ca=1, cb=0):
    return lax.dot_general(a, b, (((ca,), (cb,)), ((), ())), preferred_element_type=F32)


def kernel(
    n_dp,
    q_in,
    k_in,
    v_in,
    g_in,
    h_in,
    dq_out,
    dk_out,
    dv_out,
    wk_out,
    wv_out,
    q_buf,
    g_buf,
    kv_buf,
    q_t,
    g_t,
    e_buf,
    p_buf,
    m_buf,
    acc,
    dq_buf,
    core_send,
    core_recv,
    x_send,
    x_recv,
    fin,
    h_buf,
    kvg,
    wc_send,
    wc_recv,
    w_send,
    w_recv,
    w_res,
    s_q,
    s_g,
    s_kv,
    s_fw,
    s_h,
    s_dq,
    s_core,
    s_x,
    s_fin,
    s_a,
    s_wc,
    s_w,
    r_q,
    r_g,
    r_kv,
    r_fw,
    r_h,
    r_dq,
    r_core,
    r_x,
    r_fin,
    r_a,
    r_wc,
    r_w,
    o_sem,
):
    me_dp = lax.axis_index("dp")
    me = lax.axis_index("ctx")
    z, x, c = me // (NX * NC), (me // NC) % NX, me % NC
    oc = 1 - c
    tok = q_in.shape[0]
    blk = tok * NC
    heads = q_in.shape[1] // HD
    per_dev = heads // (NZ * NC)
    kv_cols = k_in.shape[1]
    rows = per_dev * blk

    def ctx_dev(zz, xx, cc):
        return (me_dp, (zz * NX + xx) * NC + cc)

    def remote(src, dst, ssem, rsem, dev):
        return pltpu.make_async_remote_copy(
            src_ref=src, dst_ref=dst, send_sem=ssem, recv_sem=rsem, device_id=dev, device_id_type=MESH
        )

    def wait_bytes(ref, sem):
        pltpu.make_async_copy(ref, ref, sem).wait()

    barrier = pltpu.get_barrier_semaphore()
    n_ctx = NZ * NX * NC
    for d in range(1, n_ctx):
        pl.semaphore_signal(barrier, inc=1, device_id=(me_dp, lax.rem(me + d, n_ctx)), device_id_type=MESH)
    for d in range(1, n_dp):
        pl.semaphore_signal(barrier, inc=1, device_id=(lax.rem(me_dp + d, n_dp), me), device_id_type=MESH)
    pl.semaphore_wait(barrier, n_ctx - 1 + n_dp - 1)

    my_block = z * NX + x
    share = h_in.shape[1] // n_dp

    for dz in range(NZ):
        gz = lax.rem(z + dz, NZ)
        cols = pl.ds(pl.multiple_of(gz * HD, HD), HD)
        for dx in range(NX):
            gx = lax.rem(x + dx, NX)
            for which, src in ((0, k_in), (1, v_in)):
                dst = kv_buf.at[my_block, c, which]
                if dz == 0 and dx == 0:
                    pltpu.make_async_copy(src.at[:, cols], dst, r_kv.at[my_block]).start()
                else:
                    remote(src.at[:, cols], dst, s_kv, r_kv.at[my_block], ctx_dev(gz, gx, c)).start()

    def send_queries(dz):
        gz = lax.rem(z + dz, NZ)
        for dc in range(NC):
            gc = lax.rem(c + dc, NC)
            for a in range(per_dev):
                col = ((gz * NC + gc) * per_dev + a) * HD
                cols = pl.ds(pl.multiple_of(col, HD), HD)
                spot = pl.ds(pl.multiple_of(c * tok, tok), tok)
                for src, buf, ssem, rsem in ((q_in, q_buf, s_q, r_q), (g_in, g_buf, s_g, r_g)):
                    dst = buf.at[z, a, spot, :]
                    if dz == 0 and dc == 0:
                        pltpu.make_async_copy(src.at[:, cols], dst, rsem.at[z]).start()
                    else:
                        remote(src.at[:, cols], dst, ssem, rsem.at[z], ctx_dev(gz, x, gc)).start()

    def send_far_queries():
        for dz in range(1, NZ):
            send_queries(dz)

    def send_hidden():
        for d in range(n_dp):
            gd = lax.rem(me_dp + d, n_dp)
            cols = pl.ds(pl.multiple_of(gd * share, HD), share)
            if d == 0:
                pltpu.make_async_copy(h_in.at[:, cols], h_buf.at[me_dp], r_h).start()
            else:
                remote(h_in.at[:, cols], h_buf.at[me_dp], s_h, r_h, (gd, me)).start()

    send_queries(0)
    acc[...] = jnp.zeros_like(acc)
    for d in range(NB):
        b = lax.rem(my_block + d, NB)
        wait_bytes(kv_buf.at[b, c], r_kv.at[b])
        remote(kv_buf.at[b, c], kv_buf.at[b, c], s_fw.at[b], r_fw.at[b], ctx_dev(z, x, oc)).start()
    pl.when(z >= NZ // 2)(send_far_queries)
    for d in range(NB):
        b = lax.rem(my_block + d, NB)
        wait_bytes(kv_buf.at[b, oc], r_fw.at[b])

    def over_core(zz):
        both = pl.ds(zz * NX, NX)
        return remote(core_send.at[both], core_recv.at[both], s_core.at[zz], r_core.at[zz], ctx_dev(z, x, oc))

    def over_x(zz):
        return remote(x_send.at[zz], x_recv.at[zz], s_x.at[zz], r_x.at[zz], ctx_dev(z, 1 - x, c))

    def start_core(zz):
        for b in range(zz * NX, zz * NX + NX):
            core_send[b, 0] = (acc[0, b, oc] * SCALE).astype(BF16)
            core_send[b, 1] = acc[1, b, oc].astype(BF16)
        over_core(zz).start()

    def start_x(zz):
        over_core(zz).wait_recv()
        b = zz * NX + (1 - x)
        x_send[zz, 0] = (acc[0, b, c] * SCALE + core_recv[b, 0].astype(F32)).astype(BF16)
        x_send[zz, 1] = (acc[1, b, c] + core_recv[b, 1].astype(F32)).astype(BF16)
        over_x(zz).start()

    def finish(zz):
        over_x(zz).wait_recv()
        b = zz * NX + x
        fin[zz, 0] = (
            acc[0, b, c] * SCALE + core_recv[b, 0].astype(F32) + x_recv[zz, 0].astype(F32)
        ).astype(BF16)
        fin[zz, 1] = (acc[1, b, c] + core_recv[b, 1].astype(F32) + x_recv[zz, 1].astype(F32)).astype(BF16)
        for which in range(2):
            src = fin.at[zz, which]
            dst = kvg.at[which, me_dp, :, pl.ds(pl.multiple_of(z * HD, HD), HD)]

            @pl.when(z == zz)
            def _():
                pltpu.make_async_copy(src, dst, r_fin.at[which]).start()

            @pl.when(z != zz)
            def _():
                remote(src, dst, s_fin, r_fin.at[which], ctx_dev(zz, x, c)).start()

    def attend(step, carry):
        later = NZ - step
        zq = jnp.where(step == 0, z, jnp.where(later <= z, later - 1, later))
        last = zq * NX + x
        wait_bytes(q_buf.at[zq], r_q.at[zq])
        wait_bytes(g_buf.at[zq], r_g.at[zq])
        for a in range(per_dev):
            q_t[:, a * blk : (a + 1) * blk] = q_buf[zq, a].T
            g_t[:, a * blk : (a + 1) * blk] = g_buf[zq, a].T
        qt, gt = q_t[...], g_t[...]

        def first(b, carry, masked):
            top, total, delta = carry
            at = pl.ds(pl.multiple_of(b * blk, blk), blk)
            kb = kv_buf[b, :, 0].reshape(blk, HD)
            vb = kv_buf[b, :, 1].reshape(blk, HD)
            s = dot(kb, qt) * SCALE2
            if masked:
                key_id = lax.broadcasted_iota(jnp.int32, (blk, blk), 0)
                query_id = lax.broadcasted_iota(jnp.int32, (blk, blk), 1)
                seen = key_id <= query_id
                s = jnp.concatenate(
                    [jnp.where(seen, s[:, i * blk : (i + 1) * blk], -jnp.inf) for i in range(per_dev)], 1
                )
            dp = dot(vb, gt)
            new = jnp.maximum(top, jnp.max(s, axis=0, keepdims=True))
            shrink = jnp.exp2(top - new)
            e = jnp.exp2(s - new)
            total = total * shrink + jnp.sum(e, axis=0, keepdims=True)
            delta = delta * shrink + jnp.sum(e * dp, axis=0, keepdims=True)
            e_buf[at, :] = e.astype(BF16)
            p_buf[at, :] = dp
            m_buf[pl.ds(b, 1), :] = new
            return new, total, delta

        zero = jnp.zeros((1, rows), F32)
        stats = lax.fori_loop(0, last, lambda b, t: first(b, t, False), (zero - jnp.inf, zero, zero))
        top, total, delta = first(last, stats, True)
        inv = 1.0 / total
        delta = delta * inv

        def second(b, dqt):
            at = pl.ds(pl.multiple_of(b * blk, blk), blk)
            fix = jnp.exp2(m_buf[pl.ds(b, 1), :] - top) * inv
            prob = e_buf[at, :].astype(F32) * fix
            low = prob.astype(BF16)
            ds = (prob * (p_buf[at, :] - delta)).astype(BF16)
            kb = kv_buf[b, :, 0].reshape(blk, HD)
            acc[0, b] += dot(ds, q_buf[zq].reshape(rows, HD)).reshape(NC, tok, HD)
            acc[1, b] += dot(low, g_buf[zq].reshape(rows, HD)).reshape(NC, tok, HD)
            return dqt + dot(kb.T, ds)

        dqt = lax.fori_loop(0, last + 1, second, jnp.zeros((HD, rows), F32))
        for a in range(per_dev):
            dq_buf[zq, a] = (dqt[:, a * blk : (a + 1) * blk] * SCALE).T.astype(BF16)
        for gc in range(NC):
            mine = jnp.logical_and(zq == z, c == gc)
            for a in range(per_dev):
                col = ((z * NC + c) * per_dev + a) * HD
                cols = pl.ds(pl.multiple_of(col, HD), HD)
                src = dq_buf.at[zq, a, gc * tok : (gc + 1) * tok, :]

                @pl.when(mine)
                def _():
                    pltpu.make_async_copy(src, dq_out.at[:, cols], r_dq).start()

                @pl.when(jnp.logical_not(mine))
                def _():
                    remote(src, dq_out.at[:, cols], s_dq, r_dq, ctx_dev(zq, x, gc)).start()

        pl.when(jnp.logical_and(step == 0, z < NZ // 2))(send_far_queries)

        @pl.when(step == 1)
        def _():
            start_core(NZ - 1)
            send_hidden()

        @pl.when(step == 2)
        def _():
            start_core(NZ - 2)
            start_x(NZ - 1)

        return carry

    lax.fori_loop(0, NZ, attend, 0)
    start_core(0)
    start_core(1)
    start_x(2)
    start_x(0)
    start_x(1)
    for zz in range(NZ - 1, -1, -1):
        finish(zz)

    half = tok // 2
    y, xl = me_dp // 2, me_dp % 2
    n_y = n_dp // 2
    up_y, down_y, far_y = lax.rem(y + 1, n_y), lax.rem(y + n_y - 1, n_y), lax.rem(y + 2, n_y)
    partner, up, down = y * 2 + (1 - xl), up_y * 2 + xl, down_y * 2 + xl
    up_p, down_p = up_y * 2 + (1 - xl), down_y * 2 + (1 - xl)
    low_half, high_half = pl.ds(0, half), pl.ds(half, half)
    every = pl.ds(0, tok)

    def pass_on(h, source, part, to, n):
        spot = kvg.at[h, source, part, :]
        return remote(spot, spot, s_a.at[h, n], r_a.at[h, n], (to, me))

    def hop(h, n):
        return (
            lambda: pass_on(h, me_dp, every, partner, 0),
            lambda: pass_on(h, me_dp, every, up, 1),
            lambda: pass_on(h, me_dp, every, down, 2),
            lambda: pass_on(h, partner, every, up, 3),
            lambda: pass_on(h, partner, every, down, 4),
            lambda: pass_on(h, down, low_half, up, 5),
            lambda: pass_on(h, up, high_half, down, 6),
            lambda: pass_on(h, down_p, low_half, up, 7),
            lambda: pass_on(h, up_p, high_half, down, 8),
        )[n]()

    def arrived(h, n):
        far, far_p = far_y * 2 + xl, far_y * 2 + (1 - xl)
        source, part = (
            (partner, every),
            (down, every),
            (up, every),
            (down_p, every),
            (up_p, every),
            (far, low_half),
            (far, high_half),
            (far_p, low_half),
            (far_p, high_half),
        )[n]
        wait_bytes(kvg.at[h, source, part, :], r_a.at[h, n])

    def own(h):
        wait_bytes(kvg.at[h, me_dp], r_fin.at[h])
        for n in range(3):
            hop(h, n).start()
        out = pltpu.make_async_copy(kvg.at[h, me_dp], (dk_out, dv_out)[h], o_sem.at[h])
        out.start()

    def relay(h, n, sends):
        arrived(h, n)
        for m in sends:
            hop(h, m).start()

    out_rows = share // (NB * NC)
    n_tok = n_dp * tok

    def project(h):
        cols = slice(h * kv_cols, (h + 1) * kv_cols)
        grads = kvg[h].reshape(n_tok, kv_cols)
        step_rows = share // NZ
        for i in range(NZ):
            at = slice(i * step_rows, (i + 1) * step_rows)
            p_buf[at, cols] = dot(e_buf[at, 0:n_tok], grads)
        for b in range(NB):
            at = pl.ds(pl.multiple_of((b * NC + oc) * out_rows, out_rows), out_rows)
            wc_send[h, b] = p_buf[at, cols].astype(BF16)
        w_core(h).start()

    def w_core(h):
        return remote(wc_send.at[h], wc_recv.at[h], s_wc.at[h], r_wc.at[h], ctx_dev(z, x, oc))

    def partial_sum(h, b):
        at = pl.ds(pl.multiple_of((b * NC + c) * out_rows, out_rows), out_rows)
        return p_buf[at, h * kv_cols : (h + 1) * kv_cols] + wc_recv[h, b].astype(F32)

    def spread(h):
        w_core(h).wait_recv()
        for d in range(1, NB):
            b = lax.rem(my_block + d, NB)
            w_send[h, b] = partial_sum(h, b).astype(BF16)
            dev = ctx_dev(b // NX, lax.rem(b, NX), c)
            remote(w_send.at[h, b], w_recv.at[h, my_block], s_w.at[h], r_w.at[h, my_block], dev).start()

    def collect(h):
        total = partial_sum(h, my_block)
        for d in range(1, NB):
            b = lax.rem(my_block + d, NB)
            wait_bytes(w_recv.at[h, b], r_w.at[h, b])
            total = total + w_recv[h, b].astype(F32)
        w_res[h] = total
        pltpu.make_async_copy(w_res.at[h], (wk_out, wv_out)[h], o_sem.at[2 + h]).start()

    own(0)
    wait_bytes(h_buf, r_h)
    for d in range(0, n_dp, 2):
        e_buf[0:share, d * tok : (d + 2) * tok] = h_buf[d : d + 2].reshape(2 * tok, share).T
    relay(0, 0, (3, 4))
    own(1)
    relay(0, 1, (5,))
    relay(0, 2, (6,))
    relay(1, 0, (3, 4))
    relay(0, 3, (7,))
    relay(0, 4, (8,))
    relay(1, 1, (5,))
    relay(1, 2, (6,))
    for n in range(5, 9):
        arrived(0, n)
    project(0)
    relay(1, 3, (7,))
    relay(1, 4, (8,))
    spread(0)
    for n in range(5, 9):
        arrived(1, n)
    project(1)
    spread(1)
    collect(0)
    collect(1)

    wait_bytes(dq_out, r_dq)
    part = heads - per_dev
    wait_bytes(q_in.at[:, : part * HD], s_q)
    wait_bytes(g_in.at[:, : part * HD], s_g)
    wait_bytes(q_in.at[:, : part * HD], s_dq)
    wait_bytes(q_in.at[:, : (NB - 1) * 2 * HD], s_kv)
    for b in range(NB):
        wait_bytes(kv_buf.at[b, c], s_fw.at[b])
    wait_bytes(h_in.at[:, : (n_dp - 1) * share], s_h)
    for zz in range(NZ):
        over_core(zz).wait_send()
        over_x(zz).wait_send()
    wait_bytes(fin.at[pl.ds(0, NZ - 1)], s_fin)
    for h in range(2):
        for n in range(9):
            hop(h, n).wait_send()
        w_core(h).wait_send()
        wait_bytes(w_send.at[h, pl.ds(0, NB - 1)], s_w.at[h])
        wait_bytes(kvg.at[h, me_dp], o_sem.at[h])
        wait_bytes(w_res.at[h], o_sem.at[2 + h])


def copy_out(*refs):
    sems = refs[-1]
    n = (len(refs) - 1) // 2
    copies = [pltpu.make_async_copy(refs[i], refs[n + i], sems.at[i]) for i in range(n)]
    for copy in copies:
        copy.start()
    for copy in copies:
        copy.wait()


def on_device(n_dp, queries, keys, values, out_grad, hidden):
    tok, width = queries.shape
    kv_cols = keys.shape[1]
    blk = tok * NC
    per_dev = width // HD // (NZ * NC)
    rows = per_dev * blk
    share = hidden.shape[1] // n_dp
    out_rows = share // (NZ * NX * NC)
    dma = pltpu.SemaphoreType.DMA
    any_spec = pl.BlockSpec(memory_space=pl.ANY)
    assert n_dp * tok <= rows and share <= NB * blk and 2 * kv_cols <= rows and n_dp == 8
    shapes = [
        jax.ShapeDtypeStruct(queries.shape, BF16),
        jax.ShapeDtypeStruct(keys.shape, BF16),
        jax.ShapeDtypeStruct(values.shape, BF16),
        jax.ShapeDtypeStruct((out_rows, kv_cols), F32),
        jax.ShapeDtypeStruct((out_rows, kv_cols), F32),
    ]
    results = pl.pallas_call(
        functools.partial(kernel, n_dp),
        out_shape=shapes,
        in_specs=[any_spec] * 5,
        out_specs=[any_spec] * 5,
        scratch_shapes=[
            pltpu.VMEM((NZ, per_dev, blk, HD), BF16),
            pltpu.VMEM((NZ, per_dev, blk, HD), BF16),
            pltpu.VMEM((NB, NC, 2, tok, HD), BF16),
            pltpu.VMEM((HD, rows), BF16),
            pltpu.VMEM((HD, rows), BF16),
            pltpu.VMEM((NB * blk, rows), BF16),
            pltpu.VMEM((NB * blk, rows), F32),
            pltpu.VMEM((NB, rows), F32),
            pltpu.VMEM((2, NB, NC, tok, HD), F32),
            pltpu.VMEM((NZ, per_dev, blk, HD), BF16),
            pltpu.VMEM((NB, 2, tok, HD), BF16),
            pltpu.VMEM((NB, 2, tok, HD), BF16),
            pltpu.VMEM((NZ, 2, tok, HD), BF16),
            pltpu.VMEM((NZ, 2, tok, HD), BF16),
            pltpu.VMEM((NZ, 2, tok, HD), BF16),
            pltpu.VMEM((n_dp, tok, share), BF16),
            pltpu.VMEM((2, n_dp, tok, kv_cols), BF16),
            pltpu.VMEM((2, NB, out_rows, kv_cols), BF16),
            pltpu.VMEM((2, NB, out_rows, kv_cols), BF16),
            pltpu.VMEM((2, NB, out_rows, kv_cols), BF16),
            pltpu.VMEM((2, NB, out_rows, kv_cols), BF16),
            pltpu.VMEM((2, out_rows, kv_cols), F32),
            dma,
            dma,
            dma,
            dma((NB,)),
            dma,
            dma,
            dma((NZ,)),
            dma((NZ,)),
            dma,
            dma((2, 9)),
            dma((2,)),
            dma((2,)),
            dma((NZ,)),
            dma((NZ,)),
            dma((NB,)),
            dma((NB,)),
            dma,
            dma,
            dma((NZ,)),
            dma((NZ,)),
            dma((2,)),
            dma((2, 9)),
            dma((2,)),
            dma((2, NB)),
            dma((4,)),
        ],
        compiler_params=pltpu.CompilerParams(
            collective_id=0, has_side_effects=True, vmem_limit_bytes=60 * 1024 * 1024
        ),
        cost_estimate=pl.CostEstimate(
            flops=40_000_000_000, bytes_accessed=20_000_000, transcendentals=10_000_000
        ),
        name="attention_backward",
    )(queries, keys, values, out_grad, hidden)
    return pl.pallas_call(
        copy_out,
        out_shape=shapes,
        in_specs=[any_spec] * 5,
        out_specs=[any_spec] * 5,
        scratch_shapes=[dma((5,))],
        cost_estimate=pl.CostEstimate(flops=0, bytes_accessed=4_500_000, transcendentals=0),
        name="copy_out",
    )(*results)


def solution(mesh):
    spec = P(("dp", "ctx"), None)
    return jax.shard_map(
        functools.partial(on_device, mesh.shape["dp"]),
        mesh=mesh,
        in_specs=(spec,) * 5,
        out_specs=(spec,) * 5,
        check_vma=False,
    )
```

time: 182 us -> 239 us (1.31); the launches traced: 181 us -> 235 us
  Pallas kernels: 175 us -> 234 us
  local copies, waits for them, and re-layouts: 5.45 us -> 0 us
    pallas_call x1 -> x2, Pallas kernels: 175 us -> 234 us  [the longest x1 166 us: on_device(): pl.pallas_call(functools.partial(kernel, n_dp), out_shape=shapes, in_spec...]
    unnamed x13 -> x0, local copies, waits for them, and re-layouts: 5.45 us -> none
where the time goes in v2:
time: 239 us; the launch traced here: 235 us
  Pallas kernels  234 us (98%)
    pallas_call x1, Pallas kernels, on_device(): pl.pallas_call(functools.partial(kernel, n_dp), out_shape=shapes, in_spec...  166 us
    pallas_call x1, Pallas kernels, on_device(): pl.pallas_call(copy_out, out_shape=shapes, in_specs=[any_spec] * 5, out_s...  68.6 us

profile of v2, /device:TPU:1, one launch (start us, length us, event | category | flops | bytes accessed | tf_op | source)
XLA Modules:
  0.0 235.0 jit_solution(15049820891838833540)
XLA Ops:
  0.6 165.7 %attention_backward.1 = (bf16[192,4096]{1,0:T(8,128)(2,1)}, bf16[192,512]{1,0:T(8,128)(2,1)}, bf16[192,512]{1,0:T(8,128)(2,1)}, f32[64,512]{1,0:T(8,128)}, f32[64,512]{1,0:T(8,128)}) custom-call(bf16[192,4096]{1,0:T(8,128)(2,1)} %q_in.1, bf16[192,512]{1,0:T(8,128)(2,1)} %k_in.1, bf16[192,512]{1,0:T(8,128)(2,1)} %v_in.1, bf16[192,4096]{1,0:T(8,128)(2,1)} %g_in.1, ...), custom_call_target="tpu_custom_call" | custom-call | flops 40000000000 | bytes 20000000 | tf_op jit(solution)/shard_map/attention_backward/pallas_call | solution.py:468
  166.3 68.6 %copy_out.1 = (bf16[192,4096]{1,0:T(8,128)(2,1)}, bf16[192,512]{1,0:T(8,128)(2,1)}, bf16[192,512]{1,0:T(8,128)(2,1)}, f32[64,512]{1,0:T(8,128)}, f32[64,512]{1,0:T(8,128)}) custom-call(bf16[192,4096]{1,0:T(8,128)(2,1)} %get-tuple-element.10.refs_0_, bf16[192,512]{1,0:T(8,128)(2,1)} %get-tuple-element.11.refs_1_, bf16[192,512]{1,0:T(8,128)(2,1)} %get-tuple-element.12.refs_2_, ...), custom_call_target="tpu_custom_call" | custom-call | bytes 4500000 | tf_op jit(solution)/shard_map/copy_out/pallas_call | solution.py:530

commit v3 on v2

--- a/solution.py
+++ b/solution.py
@@ -141,9 +141,12 @@
                     else:
                         remote(src.at[:, cols], dst, ssem, rsem.at[z], ctx_dev(gz, x, gc)).start()
 
-    def send_far_queries():
-        for dz in range(1, NZ):
-            send_queries(dz)
+    def send_near():
+        send_queries(1)
+        send_queries(NZ - 1)
+
+    def send_far():
+        send_queries(2)
 
     def send_hidden():
         for d in range(n_dp):
@@ -155,12 +158,13 @@
                 remote(h_in.at[:, cols], h_buf.at[me_dp], s_h, r_h, (gd, me)).start()
 
     send_queries(0)
+    send_near()
     acc[...] = jnp.zeros_like(acc)
     for d in range(NB):
         b = lax.rem(my_block + d, NB)
         wait_bytes(kv_buf.at[b, c], r_kv.at[b])
         remote(kv_buf.at[b, c], kv_buf.at[b, c], s_fw.at[b], r_fw.at[b], ctx_dev(z, x, oc)).start()
-    pl.when(z >= NZ // 2)(send_far_queries)
+    send_far()
     for d in range(NB):
         b = lax.rem(my_block + d, NB)
         wait_bytes(kv_buf.at[b, oc], r_fw.at[b])
@@ -207,6 +211,7 @@
     def attend(step, carry):
         later = NZ - step
         zq = jnp.where(step == 0, z, jnp.where(later <= z, later - 1, later))
+        zq = jnp.where(z == 1, lax.rem(step + 1, NZ), zq)
         last = zq * NX + x
         wait_bytes(q_buf.at[zq], r_q.at[zq])
         wait_bytes(g_buf.at[zq], r_g.at[zq])
@@ -274,15 +279,11 @@
                 def _():
                     remote(src, dq_out.at[:, cols], s_dq, r_dq, ctx_dev(zq, x, gc)).start()
 
-        pl.when(jnp.logical_and(step == 0, z < NZ // 2))(send_far_queries)
-
-        @pl.when(step == 1)
+        pl.when(step == 0)(send_hidden)
+
+        @pl.when(step == 2)
         def _():
             start_core(NZ - 1)
-            send_hidden()
-
-        @pl.when(step == 2)
-        def _():
             start_core(NZ - 2)
             start_x(NZ - 1)
 
@@ -438,13 +439,9 @@
 
 
 def copy_out(*refs):
-    sems = refs[-1]
-    n = (len(refs) - 1) // 2
-    copies = [pltpu.make_async_copy(refs[i], refs[n + i], sems.at[i]) for i in range(n)]
-    for copy in copies:
-        copy.start()
-    for copy in copies:
-        copy.wait()
+    n = len(refs) // 2
+    for i in range(n):
+        refs[n + i][...] = refs[i][...]
 
 
 def on_device(n_dp, queries, keys, values, out_grad, hidden):
@@ -527,12 +524,14 @@
         ),
         name="attention_backward",
     )(queries, keys, values, out_grad, hidden)
+    steps = 4
+    specs = [pl.BlockSpec((a.shape[0] // steps, a.shape[1]), lambda i: (i, 0)) for a in shapes]
     return pl.pallas_call(
         copy_out,
+        grid=(steps,),
         out_shape=shapes,
-        in_specs=[any_spec] * 5,
-        out_specs=[any_spec] * 5,
-        scratch_shapes=[dma((5,))],
+        in_specs=specs,
+        out_specs=specs,
         cost_estimate=pl.CostEstimate(flops=0, bytes_accessed=4_500_000, transcendentals=0),
         name="copy_out",
     )(*results)

time: 239 us -> 155 us (0.65); the launches traced: 235 us -> 154 us
  Pallas kernels: 234 us -> 154 us
    pallas_call x1, Pallas kernels: 68.6 us -> 3.8 us  [on_device(): pl.pallas_call(copy_out, grid=(steps,), out_shape=shapes, in_specs=specs,...]
    pallas_call x1, Pallas kernels: 166 us -> 150 us  [on_device(): pl.pallas_call(functools.partial(kernel, n_dp), out_shape=shapes, in_spec...]
where the time goes in v3:
time: 155 us; the launch traced here: 154 us
  Pallas kernels  154 us (99%)
    pallas_call x1, Pallas kernels, on_device(): pl.pallas_call(functools.partial(kernel, n_dp), out_shape=shapes, in_spec...  150 us
    pallas_call x1, Pallas kernels, on_device(): pl.pallas_call(copy_out, grid=(steps,), out_shape=shapes, in_specs=specs,...  3.8 us

profile of v3, /device:TPU:1, one launch (start us, length us, event | category | flops | bytes accessed | tf_op | source)
XLA Modules:
  0.0 154.5 jit_solution(8667337411162872133)
XLA Ops:
  0.6 150.1 %attention_backward.1 = (bf16[192,4096]{1,0:T(8,128)(2,1)}, bf16[192,512]{1,0:T(8,128)(2,1)}, bf16[192,512]{1,0:T(8,128)(2,1)}, f32[64,512]{1,0:T(8,128)}, f32[64,512]{1,0:T(8,128)}) custom-call(bf16[192,4096]{1,0:T(8,128)(2,1)} %q_in.1, bf16[192,512]{1,0:T(8,128)(2,1)} %k_in.1, bf16[192,512]{1,0:T(8,128)(2,1)} %v_in.1, bf16[192,4096]{1,0:T(8,128)(2,1)} %g_in.1, ...), custom_call_target="tpu_custom_call" | custom-call | flops 40000000000 | bytes 20000000 | tf_op jit(solution)/shard_map/attention_backward/pallas_call | solution.py:465
  150.7 3.8 %copy_out.1 = (bf16[192,4096]{1,0:T(8,128)(2,1)}, bf16[192,512]{1,0:T(8,128)(2,1)}, bf16[192,512]{1,0:T(8,128)(2,1)}, f32[64,512]{1,0:T(8,128)}, f32[64,512]{1,0:T(8,128)}) custom-call(bf16[192,4096]{1,0:T(8,128)(2,1)} %get-tuple-element.10.refs_0_, bf16[192,512]{1,0:T(8,128)(2,1)} %get-tuple-element.11.refs_1_, bf16[192,512]{1,0:T(8,128)(2,1)} %get-tuple-element.12.refs_2_, ...), custom_call_target="tpu_custom_call" | custom-call | bytes 4500000 | tf_op jit(solution)/shard_map/copy_out/pallas_call | solution.py:529

commit v4 on v3

--- a/solution.py
+++ b/solution.py
@@ -42,7 +42,7 @@
     p_buf,
     m_buf,
     acc,
-    dq_buf,
+    dq_acc,
     core_send,
     core_recv,
     x_send,
@@ -50,9 +50,7 @@
     fin,
     h_buf,
     kvg,
-    wc_send,
     wc_recv,
-    w_send,
     w_recv,
     w_res,
     s_q,
@@ -250,26 +248,41 @@
         inv = 1.0 / total
         delta = delta * inv
 
-        def second(b, dqt):
-            at = pl.ds(pl.multiple_of(b * blk, blk), blk)
-            fix = jnp.exp2(m_buf[pl.ds(b, 1), :] - top) * inv
-            prob = e_buf[at, :].astype(F32) * fix
-            low = prob.astype(BF16)
-            ds = (prob * (p_buf[at, :] - delta)).astype(BF16)
-            kb = kv_buf[b, :, 0].reshape(blk, HD)
-            acc[0, b] += dot(ds, q_buf[zq].reshape(rows, HD)).reshape(NC, tok, HD)
-            acc[1, b] += dot(low, g_buf[zq].reshape(rows, HD)).reshape(NC, tok, HD)
-            return dqt + dot(kb.T, ds)
-
-        dqt = lax.fori_loop(0, last + 1, second, jnp.zeros((HD, rows), F32))
+        def second(b, n):
+            lows, grads = [], []
+            for i in range(n):
+                at = pl.ds(pl.multiple_of((b + i) * blk, blk), blk)
+                fix = jnp.exp2(m_buf[pl.ds(b + i, 1), :] - top) * inv
+                prob = e_buf[at, :].astype(F32) * fix
+                lows.append(prob.astype(BF16))
+                grads.append((prob * (p_buf[at, :] - delta)).astype(BF16))
+            low, ds = jnp.concatenate(lows, 0), jnp.concatenate(grads, 0)
+            some = pl.ds(b, n)
+            kb = kv_buf[some, :, 0].reshape(n * blk, HD)
+            acc[0, some] += dot(ds, q_buf[zq].reshape(rows, HD)).reshape(n, NC, tok, HD)
+            acc[1, some] += dot(low, g_buf[zq].reshape(rows, HD)).reshape(n, NC, tok, HD)
+            dq_acc[...] += dot(kb.T, ds)
+
+        dq_acc[...] = jnp.zeros_like(dq_acc)
+
+        def pair(i, carry):
+            second(2 * i, 2)
+            return carry
+
+        lax.fori_loop(0, (last + 1) // 2, pair, 0)
+
+        @pl.when(x == 0)
+        def _():
+            second(last, 1)
+
         for a in range(per_dev):
-            dq_buf[zq, a] = (dqt[:, a * blk : (a + 1) * blk] * SCALE).T.astype(BF16)
+            q_buf[zq, a] = (dq_acc[:, a * blk : (a + 1) * blk] * SCALE).T.astype(BF16)
         for gc in range(NC):
             mine = jnp.logical_and(zq == z, c == gc)
             for a in range(per_dev):
                 col = ((z * NC + c) * per_dev + a) * HD
                 cols = pl.ds(pl.multiple_of(col, HD), HD)
-                src = dq_buf.at[zq, a, gc * tok : (gc + 1) * tok, :]
+                src = q_buf.at[zq, a, gc * tok : (gc + 1) * tok, :]
 
                 @pl.when(mine)
                 def _():
@@ -354,6 +367,9 @@
     out_rows = share // (NB * NC)
     n_tok = n_dp * tok
 
+    def outgoing(h, n):
+        return h_buf.at[:, n * out_rows : (n + 1) * out_rows, h * kv_cols : (h + 1) * kv_cols]
+
     def project(h):
         cols = slice(h * kv_cols, (h + 1) * kv_cols)
         grads = kvg[h].reshape(n_tok, kv_cols)
@@ -363,11 +379,11 @@
             p_buf[at, cols] = dot(e_buf[at, 0:n_tok], grads)
         for b in range(NB):
             at = pl.ds(pl.multiple_of((b * NC + oc) * out_rows, out_rows), out_rows)
-            wc_send[h, b] = p_buf[at, cols].astype(BF16)
+            outgoing(h, 0)[b] = p_buf[at, cols].astype(BF16)
         w_core(h).start()
 
     def w_core(h):
-        return remote(wc_send.at[h], wc_recv.at[h], s_wc.at[h], r_wc.at[h], ctx_dev(z, x, oc))
+        return remote(outgoing(h, 0), wc_recv.at[h], s_wc.at[h], r_wc.at[h], ctx_dev(z, x, oc))
 
     def partial_sum(h, b):
         at = pl.ds(pl.multiple_of((b * NC + c) * out_rows, out_rows), out_rows)
@@ -377,9 +393,9 @@
         w_core(h).wait_recv()
         for d in range(1, NB):
             b = lax.rem(my_block + d, NB)
-            w_send[h, b] = partial_sum(h, b).astype(BF16)
+            outgoing(h, 1)[b] = partial_sum(h, b).astype(BF16)
             dev = ctx_dev(b // NX, lax.rem(b, NX), c)
-            remote(w_send.at[h, b], w_recv.at[h, my_block], s_w.at[h], r_w.at[h, my_block], dev).start()
+            remote(outgoing(h, 1).at[b], w_recv.at[h, my_block], s_w.at[h], r_w.at[h, my_block], dev).start()
 
     def collect(h):
         total = partial_sum(h, my_block)
@@ -433,7 +449,7 @@
         for n in range(9):
             hop(h, n).wait_send()
         w_core(h).wait_send()
-        wait_bytes(w_send.at[h, pl.ds(0, NB - 1)], s_w.at[h])
+        wait_bytes(w_recv.at[h, pl.ds(0, NB - 1)], s_w.at[h])
         wait_bytes(kvg.at[h, me_dp], o_sem.at[h])
         wait_bytes(w_res.at[h], o_sem.at[2 + h])
 
@@ -454,7 +470,7 @@
     out_rows = share // (NZ * NX * NC)
     dma = pltpu.SemaphoreType.DMA
     any_spec = pl.BlockSpec(memory_space=pl.ANY)
-    assert n_dp * tok <= rows and share <= NB * blk and 2 * kv_cols <= rows and n_dp == 8
+    assert n_dp * tok <= rows and share <= NB * blk and 2 * kv_cols <= rows and n_dp == NB == 8
     shapes = [
         jax.ShapeDtypeStruct(queries.shape, BF16),
         jax.ShapeDtypeStruct(keys.shape, BF16),
@@ -477,7 +493,7 @@
             pltpu.VMEM((NB * blk, rows), F32),
             pltpu.VMEM((NB, rows), F32),
             pltpu.VMEM((2, NB, NC, tok, HD), F32),
-            pltpu.VMEM((NZ, per_dev, blk, HD), BF16),
+            pltpu.VMEM((HD, rows), F32),
             pltpu.VMEM((NB, 2, tok, HD), BF16),
             pltpu.VMEM((NB, 2, tok, HD), BF16),
             pltpu.VMEM((NZ, 2, tok, HD), BF16),
@@ -485,8 +501,6 @@
             pltpu.VMEM((NZ, 2, tok, HD), BF16),
             pltpu.VMEM((n_dp, tok, share), BF16),
             pltpu.VMEM((2, n_dp, tok, kv_cols), BF16),
-            pltpu.VMEM((2, NB, out_rows, kv_cols), BF16),
-            pltpu.VMEM((2, NB, out_rows, kv_cols), BF16),
             pltpu.VMEM((2, NB, out_rows, kv_cols), BF16),
             pltpu.VMEM((2, NB, out_rows, kv_cols), BF16),
             pltpu.VMEM((2, out_rows, kv_cols), F32),

time: 155 us -> 151 us (0.974)
  Pallas kernels: 154 us -> 150 us
    pallas_call x1, Pallas kernels: 150 us -> 146 us  [on_device(): pl.pallas_call(functools.partial(kernel, n_dp), out_shape=shapes, in_spec...]
where the time goes in v4:
time: 151 us; the launch traced here: 150 us
  Pallas kernels  150 us (99%)
    pallas_call x1, Pallas kernels, on_device(): pl.pallas_call(functools.partial(kernel, n_dp), out_shape=shapes, in_spec...  146 us
    pallas_call x1, Pallas kernels, on_device(): pl.pallas_call(copy_out, grid=(steps,), out_shape=shapes, in_specs=specs,...  3.8 us

profile of v4, /device:TPU:1, one launch (start us, length us, event | category | flops | bytes accessed | tf_op | source)
XLA Modules:
  0.0 150.4 jit_solution(7111068476407292832)
XLA Ops:
  0.6 145.9 %attention_backward.1 = (bf16[192,4096]{1,0:T(8,128)(2,1)}, bf16[192,512]{1,0:T(8,128)(2,1)}, bf16[192,512]{1,0:T(8,128)(2,1)}, f32[64,512]{1,0:T(8,128)}, f32[64,512]{1,0:T(8,128)}) custom-call(bf16[192,4096]{1,0:T(8,128)(2,1)} %q_in.1, bf16[192,512]{1,0:T(8,128)(2,1)} %k_in.1, bf16[192,512]{1,0:T(8,128)(2,1)} %v_in.1, bf16[192,4096]{1,0:T(8,128)(2,1)} %g_in.1, ...), custom_call_target="tpu_custom_call" | custom-call | flops 40000000000 | bytes 20000000 | tf_op jit(solution)/shard_map/attention_backward/pallas_call | solution.py:481
  146.6 3.8 %copy_out.1 = (bf16[192,4096]{1,0:T(8,128)(2,1)}, bf16[192,512]{1,0:T(8,128)(2,1)}, bf16[192,512]{1,0:T(8,128)(2,1)}, f32[64,512]{1,0:T(8,128)}, f32[64,512]{1,0:T(8,128)}) custom-call(bf16[192,4096]{1,0:T(8,128)(2,1)} %get-tuple-element.10.refs_0_, bf16[192,512]{1,0:T(8,128)(2,1)} %get-tuple-element.11.refs_1_, bf16[192,512]{1,0:T(8,128)(2,1)} %get-tuple-element.12.refs_2_, ...), custom_call_target="tpu_custom_call" | custom-call | bytes 4500000 | tf_op jit(solution)/shard_map/copy_out/pallas_call | solution.py:543

commit v5 on v4

--- a/solution.py
+++ b/solution.py
@@ -308,8 +308,12 @@
     start_x(2)
     start_x(0)
     start_x(1)
+    wait_bytes(h_buf, r_h)
     for zz in range(NZ - 1, -1, -1):
         finish(zz)
+        if zz >= 2:
+            for d in range(4 * (NZ - 1 - zz), 4 * (NZ - zz), 2):
+                e_buf[0:share, d * tok : (d + 2) * tok] = h_buf[d : d + 2].reshape(2 * tok, share).T
 
     half = tok // 2
     y, xl = me_dp // 2, me_dp % 2
@@ -329,8 +333,8 @@
             lambda: pass_on(h, me_dp, every, partner, 0),
             lambda: pass_on(h, me_dp, every, up, 1),
             lambda: pass_on(h, me_dp, every, down, 2),
-            lambda: pass_on(h, partner, every, up, 3),
-            lambda: pass_on(h, partner, every, down, 4),
+            lambda: pass_on(h, partner, every, up, 3) if h == 0 else pass_on(h, down, every, partner, 3),
+            lambda: pass_on(h, partner, every, down, 4) if h == 1 else pass_on(h, up, every, partner, 4),
             lambda: pass_on(h, down, low_half, up, 5),
             lambda: pass_on(h, up, high_half, down, 6),
             lambda: pass_on(h, down_p, low_half, up, 7),
@@ -407,18 +411,15 @@
         pltpu.make_async_copy(w_res.at[h], (wk_out, wv_out)[h], o_sem.at[2 + h]).start()
 
     own(0)
-    wait_bytes(h_buf, r_h)
-    for d in range(0, n_dp, 2):
-        e_buf[0:share, d * tok : (d + 2) * tok] = h_buf[d : d + 2].reshape(2 * tok, share).T
-    relay(0, 0, (3, 4))
+    relay(0, 0, (3,))
     own(1)
     relay(0, 1, (5,))
-    relay(0, 2, (6,))
-    relay(1, 0, (3, 4))
+    relay(0, 2, (6, 4))
+    relay(1, 0, (4,))
     relay(0, 3, (7,))
+    relay(1, 1, (5, 3))
+    relay(1, 2, (6,))
     relay(0, 4, (8,))
-    relay(1, 1, (5,))
-    relay(1, 2, (6,))
     for n in range(5, 9):
         arrived(0, n)
     project(0)

time: 151 us -> 148 us (0.980)
  Pallas kernels: 150 us -> 147 us
    pallas_call x1, Pallas kernels: 146 us -> 143 us  [on_device(): pl.pallas_call(functools.partial(kernel, n_dp), out_shape=shapes, in_spec...]
where the time goes in v5:
time: 148 us; the launch traced here: 147 us
  Pallas kernels  147 us (99%)
    pallas_call x1, Pallas kernels, on_device(): pl.pallas_call(functools.partial(kernel, n_dp), out_shape=shapes, in_spec...  143 us
    pallas_call x1, Pallas kernels, on_device(): pl.pallas_call(copy_out, grid=(steps,), out_shape=shapes, in_specs=specs,...  3.8 us

profile of v5, /device:TPU:1, one launch (start us, length us, event | category | flops | bytes accessed | tf_op | source)
XLA Modules:
  0.0 147.5 jit_solution(10307115976077250590)
XLA Ops:
  0.6 143.1 %attention_backward.1 = (bf16[192,4096]{1,0:T(8,128)(2,1)}, bf16[192,512]{1,0:T(8,128)(2,1)}, bf16[192,512]{1,0:T(8,128)(2,1)}, f32[64,512]{1,0:T(8,128)}, f32[64,512]{1,0:T(8,128)}) custom-call(bf16[192,4096]{1,0:T(8,128)(2,1)} %q_in.1, bf16[192,512]{1,0:T(8,128)(2,1)} %k_in.1, bf16[192,512]{1,0:T(8,128)(2,1)} %v_in.1, bf16[192,4096]{1,0:T(8,128)(2,1)} %g_in.1, ...), custom_call_target="tpu_custom_call" | custom-call | flops 40000000000 | bytes 20000000 | tf_op jit(solution)/shard_map/attention_backward/pallas_call | solution.py:482
  143.7 3.8 %copy_out.1 = (bf16[192,4096]{1,0:T(8,128)(2,1)}, bf16[192,512]{1,0:T(8,128)(2,1)}, bf16[192,512]{1,0:T(8,128)(2,1)}, f32[64,512]{1,0:T(8,128)}, f32[64,512]{1,0:T(8,128)}) custom-call(bf16[192,4096]{1,0:T(8,128)(2,1)} %get-tuple-element.10.refs_0_, bf16[192,512]{1,0:T(8,128)(2,1)} %get-tuple-element.11.refs_1_, bf16[192,512]{1,0:T(8,128)(2,1)} %get-tuple-element.12.refs_2_, ...), custom_call_target="tpu_custom_call" | custom-call | bytes 4500000 | tf_op jit(solution)/shard_map/copy_out/pallas_call | solution.py:544

commit v6 on v5

--- a/solution.py
+++ b/solution.py
@@ -166,6 +166,7 @@
     for d in range(NB):
         b = lax.rem(my_block + d, NB)
         wait_bytes(kv_buf.at[b, oc], r_fw.at[b])
+    send_hidden()
 
     def over_core(zz):
         both = pl.ds(zz * NX, NX)
@@ -292,8 +293,6 @@
                 def _():
                     remote(src, dq_out.at[:, cols], s_dq, r_dq, ctx_dev(zq, x, gc)).start()
 
-        pl.when(step == 0)(send_hidden)
-
         @pl.when(step == 2)
         def _():
             start_core(NZ - 1)
@@ -308,9 +307,10 @@
     start_x(2)
     start_x(0)
     start_x(1)
-    wait_bytes(h_buf, r_h)
     for zz in range(NZ - 1, -1, -1):
         finish(zz)
+        if zz == NZ - 1:
+            wait_bytes(h_buf, r_h)
         if zz >= 2:
             for d in range(4 * (NZ - 1 - zz), 4 * (NZ - zz), 2):
                 e_buf[0:share, d * tok : (d + 2) * tok] = h_buf[d : d + 2].reshape(2 * tok, share).T

time: 148 us -> 148 us (level)
  no operation moved by 1% of the time
where the time goes in v6:
time: 148 us; the launch traced here: 147 us
  Pallas kernels  147 us (99%)
    pallas_call x1, Pallas kernels, on_device(): pl.pallas_call(functools.partial(kernel, n_dp), out_shape=shapes, in_spec...  143 us
    pallas_call x1, Pallas kernels, on_device(): pl.pallas_call(copy_out, grid=(steps,), out_shape=shapes, in_specs=specs,...  3.8 us

profile of v6, /device:TPU:1, one launch (start us, length us, event | category | flops | bytes accessed | tf_op | source)
XLA Modules:
  0.0 147.5 jit_solution(18147276531242806295)
XLA Ops:
  0.6 143.0 %attention_backward.1 = (bf16[192,4096]{1,0:T(8,128)(2,1)}, bf16[192,512]{1,0:T(8,128)(2,1)}, bf16[192,512]{1,0:T(8,128)(2,1)}, f32[64,512]{1,0:T(8,128)}, f32[64,512]{1,0:T(8,128)}) custom-call(bf16[192,4096]{1,0:T(8,128)(2,1)} %q_in.1, bf16[192,512]{1,0:T(8,128)(2,1)} %k_in.1, bf16[192,512]{1,0:T(8,128)(2,1)} %v_in.1, bf16[192,4096]{1,0:T(8,128)(2,1)} %g_in.1, ...), custom_call_target="tpu_custom_call" | custom-call | flops 40000000000 | bytes 20000000 | tf_op jit(solution)/shard_map/attention_backward/pallas_call | solution.py:482
  143.7 3.8 %copy_out.1 = (bf16[192,4096]{1,0:T(8,128)(2,1)}, bf16[192,512]{1,0:T(8,128)(2,1)}, bf16[192,512]{1,0:T(8,128)(2,1)}, f32[64,512]{1,0:T(8,128)}, f32[64,512]{1,0:T(8,128)}) custom-call(bf16[192,4096]{1,0:T(8,128)(2,1)} %get-tuple-element.10.refs_0_, bf16[192,512]{1,0:T(8,128)(2,1)} %get-tuple-element.11.refs_1_, bf16[192,512]{1,0:T(8,128)(2,1)} %get-tuple-element.12.refs_2_, ...), custom_call_target="tpu_custom_call" | custom-call | bytes 4500000 | tf_op jit(solution)/shard_map/copy_out/pallas_call | solution.py:544

commit v7 on v6

--- a/solution.py
+++ b/solution.py
@@ -378,28 +378,36 @@
         cols = slice(h * kv_cols, (h + 1) * kv_cols)
         grads = kvg[h].reshape(n_tok, kv_cols)
         step_rows = share // NZ
-        for i in range(NZ):
-            at = slice(i * step_rows, (i + 1) * step_rows)
+        for k in range(NZ):
+            i = lax.rem(z + k, NZ)
+            at = pl.ds(pl.multiple_of(i * step_rows, step_rows), step_rows)
             p_buf[at, cols] = dot(e_buf[at, 0:n_tok], grads)
-        for b in range(NB):
-            at = pl.ds(pl.multiple_of((b * NC + oc) * out_rows, out_rows), out_rows)
-            outgoing(h, 0)[b] = p_buf[at, cols].astype(BF16)
-        w_core(h).start()
-
-    def w_core(h):
-        return remote(outgoing(h, 0), wc_recv.at[h], s_wc.at[h], r_wc.at[h], ctx_dev(z, x, oc))
+            for xx in range(NX):
+                b = i * NX + xx
+                at = pl.ds(pl.multiple_of((b * NC + oc) * out_rows, out_rows), out_rows)
+                outgoing(h, 0)[b] = p_buf[at, cols].astype(BF16)
+            w_core(h, i).start()
+
+    def w_core(h, i):
+        some = pl.ds(i * NX, NX)
+        dst = wc_recv.at[h, some]
+        return remote(outgoing(h, 0).at[some], dst, s_wc.at[h, i], r_wc.at[h, i], ctx_dev(z, x, oc))
 
     def partial_sum(h, b):
         at = pl.ds(pl.multiple_of((b * NC + c) * out_rows, out_rows), out_rows)
         return p_buf[at, h * kv_cols : (h + 1) * kv_cols] + wc_recv[h, b].astype(F32)
 
     def spread(h):
-        w_core(h).wait_recv()
-        for d in range(1, NB):
-            b = lax.rem(my_block + d, NB)
-            outgoing(h, 1)[b] = partial_sum(h, b).astype(BF16)
-            dev = ctx_dev(b // NX, lax.rem(b, NX), c)
-            remote(outgoing(h, 1).at[b], w_recv.at[h, my_block], s_w.at[h], r_w.at[h, my_block], dev).start()
+        for k in range(NZ):
+            i = lax.rem(z + k, NZ)
+            w_core(h, i).wait_recv()
+            for xx in range(NX):
+                gx = lax.rem(x + xx, NX)
+                b = i * NX + gx
+                if k > 0 or xx > 0:
+                    outgoing(h, 1)[b] = partial_sum(h, b).astype(BF16)
+                    dst = w_recv.at[h, my_block]
+                    remote(outgoing(h, 1).at[b], dst, s_w.at[h], r_w.at[h, my_block], ctx_dev(i, gx, c)).start()
 
     def collect(h):
         total = partial_sum(h, my_block)
@@ -449,16 +457,30 @@
     for h in range(2):
         for n in range(9):
             hop(h, n).wait_send()
-        w_core(h).wait_send()
+        for i in range(NZ):
+            w_core(h, i).wait_send()
         wait_bytes(w_recv.at[h, pl.ds(0, NB - 1)], s_w.at[h])
         wait_bytes(kvg.at[h, me_dp], o_sem.at[h])
         wait_bytes(w_res.at[h], o_sem.at[2 + h])
 
 
 def copy_out(*refs):
-    n = len(refs) // 2
-    for i in range(n):
-        refs[n + i][...] = refs[i][...]
+    sources, targets, held, in_sem, out_sem = refs[:5], refs[5:10], refs[10:15], refs[15], refs[16]
+    pieces = []
+    for n in range(5):
+        steps = 4 if n == 0 else 1
+        size = sources[n].shape[0] // steps
+        for i in range(steps):
+            pieces.append((n, pl.ds(i * size, size)))
+    ins = [pltpu.make_async_copy(sources[n].at[at], held[n].at[at], in_sem.at[k]) for k, (n, at) in enumerate(pieces)]
+    outs = [pltpu.make_async_copy(held[n].at[at], targets[n].at[at], out_sem.at[k]) for k, (n, at) in enumerate(pieces)]
+    for copy in ins:
+        copy.start()
+    for first, second in zip(ins, outs):
+        first.wait()
+        second.start()
+    for copy in outs:
+        copy.wait()
 
 
 def on_device(n_dp, queries, keys, values, out_grad, hidden):
@@ -515,7 +537,7 @@
             dma((NZ,)),
             dma,
             dma((2, 9)),
-            dma((2,)),
+            dma((2, NZ)),
             dma((2,)),
             dma((NZ,)),
             dma((NZ,)),
@@ -527,26 +549,24 @@
             dma((NZ,)),
             dma((2,)),
             dma((2, 9)),
-            dma((2,)),
+            dma((2, NZ)),
             dma((2, NB)),
             dma((4,)),
         ],
         compiler_params=pltpu.CompilerParams(
-            collective_id=0, has_side_effects=True, vmem_limit_bytes=60 * 1024 * 1024
+            collective_id=0, has_side_effects=True, vmem_limit_bytes=63 * 1024 * 1024
         ),
         cost_estimate=pl.CostEstimate(
             flops=40_000_000_000, bytes_accessed=20_000_000, transcendentals=10_000_000
         ),
         name="attention_backward",
     )(queries, keys, values, out_grad, hidden)
-    steps = 4
-    specs = [pl.BlockSpec((a.shape[0] // steps, a.shape[1]), lambda i: (i, 0)) for a in shapes]
     return pl.pallas_call(
         copy_out,
-        grid=(steps,),
         out_shape=shapes,
-        in_specs=specs,
-        out_specs=specs,
+        in_specs=[any_spec] * 5,
+        out_specs=[any_spec] * 5,
+        scratch_shapes=[pltpu.VMEM(a.shape, a.dtype) for a in shapes] + [dma((8,)), dma((8,))],
         cost_estimate=pl.CostEstimate(flops=0, bytes_accessed=4_500_000, transcendentals=0),
         name="copy_out",
     )(*results)

time: 148 us -> 146 us (0.986)
  Pallas kernels: 147 us -> 145 us
where the time goes in v7:
time: 146 us; the launch traced here: 145 us
  Pallas kernels  145 us (99%)
    pallas_call x1, Pallas kernels, on_device(): pl.pallas_call(functools.partial(kernel, n_dp), out_shape=shapes, in_spec...  142 us

profile of v7, /device:TPU:1, one launch (start us, length us, event | category | flops | bytes accessed | tf_op | source)
XLA Modules:
  0.0 145.4 jit_solution(948985470151551652)
XLA Ops:
  0.6 142.3 %attention_backward.1 = (bf16[192,4096]{1,0:T(8,128)(2,1)}, bf16[192,512]{1,0:T(8,128)(2,1)}, bf16[192,512]{1,0:T(8,128)(2,1)}, f32[64,512]{1,0:T(8,128)}, f32[64,512]{1,0:T(8,128)}) custom-call(bf16[192,4096]{1,0:T(8,128)(2,1)} %q_in.1, bf16[192,512]{1,0:T(8,128)(2,1)} %k_in.1, bf16[192,512]{1,0:T(8,128)(2,1)} %v_in.1, bf16[192,4096]{1,0:T(8,128)(2,1)} %g_in.1, ...), custom_call_target="tpu_custom_call" | custom-call | flops 40000000000 | bytes 20000000 | tf_op jit(solution)/shard_map/attention_backward/pallas_call | solution.py:504
  142.9 2.5 %copy_out.1 = (bf16[192,4096]{1,0:T(8,128)(2,1)}, bf16[192,512]{1,0:T(8,128)(2,1)}, bf16[192,512]{1,0:T(8,128)(2,1)}, f32[64,512]{1,0:T(8,128)}, f32[64,512]{1,0:T(8,128)}) custom-call(bf16[192,4096]{1,0:T(8,128)(2,1)} %get-tuple-element.10.refs_0_, bf16[192,512]{1,0:T(8,128)(2,1)} %get-tuple-element.11.refs_1_, bf16[192,512]{1,0:T(8,128)(2,1)} %get-tuple-element.12.refs_2_, ...), custom_call_target="tpu_custom_call" | custom-call | bytes 4500000 | tf_op jit(solution)/shard_map/copy_out/pallas_call | solution.py:564
